TPU v7x, 32 devices: a whole 2x2x4 slice. The times are simulated.
32 devices in a mesh: ctx: 16 (over z, y, core), wsh: 2 (over x).
Axes of the slice: x: 2, y: 2, z: 4, core: 2. Of those that a mesh axis runs over, the one named last changes fastest.
Arguments:
- content: bfloat16 [2, 2048, 768], P('wsh', 'ctx')
- query_stream: bfloat16 [2, 2048, 768], P('wsh', 'ctx'), may hold values from -6 to 6
- block_rank: int32 [2, 16], P('wsh', 'ctx'), may hold values from 0 to 15, each once within a row
- segments: int32 [2, 2048], P('wsh', 'ctx'), may hold values from 0 to 3, never falling along the last dimension, each value on 1 to 1024 neighbouring positions
- positions: int32 [2, 2048], P('wsh', 'ctx'), may hold values from 0 to 2152, as said below
- query_weight: bfloat16 [768, 768], P('wsh'), may hold values from -0.21875 to 0.21875
- key_weight: bfloat16 [768, 768], P('wsh'), may hold values from -0.21875 to 0.21875
- value_weight: bfloat16 [768, 768], P('wsh'), may hold values from -0.21875 to 0.21875
- output_weight: bfloat16 [768, 768], P('wsh'), may hold values from -1.75 to 1.75
- content_bias: bfloat16 [768], P('wsh'), may hold values from -3 to 3
- segment_bias: bfloat16 [768], P('wsh'), may hold values from -3 to 3
- segment_embed: bfloat16 [2, 768], P(None, 'wsh'), may hold values from -4 to 4
- relative_table: bfloat16 [12, 33], P('wsh'), may hold values from -4 to 4
- attention_gain: bfloat16 [768], P('wsh'), may hold values from 0.5 to 1.5
- attention_shift: bfloat16 [768], P('wsh'), may hold values from -1 to 1
- inner_weight: bfloat16 [768, 3072], P('wsh'), may hold values from -0.21875 to 0.21875
- inner_bias: bfloat16 [3072], P('wsh'), may hold values from -1 to 1
- outer_weight: bfloat16 [3072, 768], P('wsh'), may hold values from -0.109375 to 0.109375
- outer_bias: bfloat16 [768], P('wsh'), may hold values from -1 to 1
- final_gain: bfloat16 [768], P('wsh'), may hold values from 0.5 to 1.5
- final_shift: bfloat16 [768], P('wsh'), may hold values from -1 to 1
- content_cotangent: bfloat16 [2, 2048, 768], P('wsh', 'ctx'), may hold values from -6 to 6
- query_cotangent: bfloat16 [2, 2048, 768], P('wsh', 'ctx'), may hold values from -6 to 6
Outputs:
- content_result: bfloat16 [2, 2048, 768], P('wsh', 'ctx')
- query_result: bfloat16 [2, 2048, 768], P('wsh', 'ctx')
- content_gradient: float32 [2, 2048, 768], P('wsh', 'ctx')
- query_gradient: float32 [2, 2048, 768], P('wsh', 'ctx')
- query_weight_gradient: float32 [768, 768], P('wsh')
- key_weight_gradient: float32 [768, 768], P('wsh')
- value_weight_gradient: float32 [768, 768], P('wsh')
- output_weight_gradient: float32 [768, 768], P('wsh')
- content_bias_gradient: float32 [768], P('wsh')
- segment_bias_gradient: float32 [768], P('wsh')
- segment_embed_gradient: float32 [2, 768], P(None, 'wsh')
- relative_table_gradient: float32 [12, 33], P('wsh')
- attention_gain_gradient: float32 [768], P('wsh')
- attention_shift_gradient: float32 [768], P('wsh')
- inner_weight_gradient: float32 [768, 3072], P('wsh')
- inner_bias_gradient: float32 [3072], P('wsh')
- outer_weight_gradient: float32 [3072, 768], P('wsh')
- outer_bias_gradient: float32 [768], P('wsh')
- final_gain_gradient: float32 [768], P('wsh')
- final_shift_gradient: float32 [768], P('wsh')
- root_mean_squares: float32 [3], replicated
Inputs may be any that keep to these rules, and one draw needn't show every extreme that they name: In each sequence positions rise by one inside each block of 128 tokens and never fall between blocks; the first token has position 0.
All inputs are finite; a program needn't handle non-finite values.
Results may differ from a plain program's by a relative error of at most 0.025.
Values may be sent and summed in bfloat16 or wider, within the bound.
No kernel may reach another device: no remote copies, remote signals or barrier semaphores. Data moves between devices by JAX's collectives and lax.ppermute only.
A program may use at most 448 MiB of HBM per device.

v0:
```python
import jax
import jax.numpy as jnp
from jax import lax
from jax.sharding import PartitionSpec as P

negative = -1e30
epsilon = 1e-05
bucket_steps = 16
key_rows = 1024
highest = lax.Precision.HIGHEST


def layer_norm(values, gain_row, shift_row):
    centred = values - jnp.mean(values, axis=-1, keepdims=True)
    spread = jnp.mean(centred * centred, axis=-1, keepdims=True)
    return centred * lax.rsqrt(spread + epsilon) * gain_row + shift_row


def gelu_exact(values):
    return jax.nn.gelu(values, approximate=False)


def bucket_levels(distance, length):
    result = jnp.full(distance.shape, bucket_steps, jnp.int32)
    for level_index in range(bucket_steps):
        bound_value = 1 + level_index * level_index * length // (bucket_steps * bucket_steps)
        result = (
            result
            + (distance >= bound_value).astype(jnp.int32)
            - (distance <= -bound_value).astype(jnp.int32)
        )
    return result


def toeplitz_band(vector, rows, cols):
    width = rows + cols - 1
    flipped = jnp.flip(vector, axis=-1)
    tiled = jnp.tile(flipped, (1,) * (vector.ndim - 1) + (rows + 1,))
    start = rows - 1
    flat = lax.slice_in_dim(tiled, start, start + rows * (width - 1), axis=vector.ndim - 1)
    return flat.reshape(vector.shape[:-1] + (rows, width - 1))[..., :cols]


def band_sums(matrix, rows, cols):
    width = rows + cols - 1
    leading = matrix.shape[:-2]
    padded = jnp.pad(matrix, [(0, 0)] * len(leading) + [(0, 0), (0, width - 1 - cols)])
    flat = padded.reshape(leading + (rows * (width - 1),))
    flat = jnp.pad(flat, [(0, 0)] * len(leading) + [(rows - 1, width + 1)])
    folded = jnp.sum(flat.reshape(leading + (rows + 1, width)), axis=-2)
    return jnp.flip(folded, axis=-1)


def allowed_pairs(row_ranks, row_streams, row_index, key_ranks, key_index):
    earlier = key_ranks[None, :] < row_ranks[:, None]
    same_block = key_ranks[None, :] == row_ranks[:, None]
    other_token = (key_index[None, :] != row_index[:, None]) | (row_streams[:, None] == 0)
    return earlier | same_block & other_token


def in_blocks(step_fn, running, portion):
    row_total = portion[0].shape[0]
    part_count = row_total // key_rows
    stacked = tuple(
        (member.reshape((part_count, key_rows) + member.shape[1:]) for member in portion)
    )
    starts = jnp.arange(part_count, dtype=jnp.int32) * key_rows

    def scan_turn(carried, scan_item):
        return (step_fn(carried, scan_item[1], scan_item[0]), None)

    final_state, unused = lax.scan(scan_turn, running, (starts, stacked))
    return final_state


def body(
    content,
    query_stream,
    block_rank,
    segments,
    positions,
    query_weight,
    key_weight,
    value_weight,
    output_weight,
    content_bias,
    segment_bias,
    segment_embed,
    relative_table,
    attention_gain,
    attention_shift,
    inner_weight,
    inner_bias,
    outer_weight,
    outer_bias,
    final_gain,
    final_shift,
    content_cotangent,
    query_cotangent,
):
    block_rows = content.shape[1]
    model_width = content.shape[2]
    row_count = 2 * block_rows
    ctx_count = lax.axis_size("ctx")
    length = block_rows * ctx_count
    gathered_weights = (
        lax.all_gather(query_weight, "wsh", axis=0, tiled=True),
        lax.all_gather(key_weight, "wsh", axis=0, tiled=True),
        lax.all_gather(value_weight, "wsh", axis=0, tiled=True),
        lax.all_gather(output_weight, "wsh", axis=0, tiled=True),
        lax.all_gather(content_bias, "wsh", axis=0, tiled=True),
        lax.all_gather(segment_bias, "wsh", axis=0, tiled=True),
        lax.all_gather(segment_embed, "wsh", axis=1, tiled=True),
        lax.all_gather(relative_table, "wsh", axis=0, tiled=True),
        lax.all_gather(attention_gain, "wsh", axis=0, tiled=True),
        lax.all_gather(attention_shift, "wsh", axis=0, tiled=True),
        lax.all_gather(inner_weight, "wsh", axis=0, tiled=True),
        lax.all_gather(inner_bias, "wsh", axis=0, tiled=True),
        lax.all_gather(outer_weight, "wsh", axis=0, tiled=True),
        lax.all_gather(outer_bias, "wsh", axis=0, tiled=True),
        lax.all_gather(final_gain, "wsh", axis=0, tiled=True),
        lax.all_gather(final_shift, "wsh", axis=0, tiled=True),
    )
    weight_query = gathered_weights[0]
    weight_key = gathered_weights[1]
    weight_value = gathered_weights[2]
    weight_output = gathered_weights[3]
    bias_content = gathered_weights[4].astype(jnp.float32)
    bias_segment = gathered_weights[5].astype(jnp.float32)
    table_full = gathered_weights[7].astype(jnp.float32)
    head_count = table_full.shape[0]
    bucket_count = table_full.shape[1]
    head_size = model_width // head_count
    embed_pair = gathered_weights[6].astype(jnp.float32).reshape(2, head_count, head_size)
    gain_first = gathered_weights[8].astype(jnp.float32)
    shift_first = gathered_weights[9].astype(jnp.float32)
    weight_inner = gathered_weights[10]
    bias_inner = gathered_weights[11].astype(jnp.float32)
    weight_outer = gathered_weights[12]
    bias_outer = gathered_weights[13].astype(jnp.float32)
    gain_second = gathered_weights[14].astype(jnp.float32)
    shift_second = gathered_weights[15].astype(jnp.float32)
    own_content = content[0]
    own_query = query_stream[0]
    streams = jnp.concatenate([own_content, own_query], axis=0)
    query_full = jnp.dot(streams, weight_query, preferred_element_type=jnp.float32)
    key_low = jnp.dot(own_content, weight_key, preferred_element_type=jnp.float32).astype(
        jnp.bfloat16
    )
    value_low = jnp.dot(own_content, weight_value, preferred_element_type=jnp.float32).astype(
        jnp.bfloat16
    )
    query_low = (
        (query_full + bias_content).astype(jnp.bfloat16).reshape(row_count, head_count, head_size)
    )
    query_shift = (query_full + bias_segment).reshape(row_count, head_count, head_size)
    seg_zero = jnp.sum(query_shift * embed_pair[0][None], axis=2).T
    seg_one = jnp.sum(query_shift * embed_pair[1][None], axis=2).T
    own_rank = block_rank[0, 0]
    rank_tokens = jnp.full((block_rows,), own_rank, jnp.int32)
    own_places = positions[0]
    own_segments = segments[0]
    token_index = lax.axis_index("ctx") * block_rows + jnp.arange(block_rows, dtype=jnp.int32)
    row_ranks = jnp.full((row_count,), own_rank, jnp.int32)
    row_streams = jnp.concatenate(
        [jnp.zeros((block_rows,), jnp.int32), jnp.ones((block_rows,), jnp.int32)]
    )
    row_index = jnp.concatenate([token_index, token_index])
    row_segments = jnp.concatenate([own_segments, own_segments])
    bucket_ids = jnp.arange(bucket_count, dtype=jnp.int32)

    def key_scores(portion, offset):
        keys_part, values_part, ranks_part, places_part, segs_part = portion
        key_count = keys_part.shape[0]
        pieces = key_count // block_rows
        key_heads = keys_part.reshape(key_count, head_count, head_size)
        value_heads = values_part.reshape(key_count, head_count, head_size)
        key_firsts = places_part.reshape(pieces, block_rows)[:, 0]
        diagonal = jnp.arange(block_rows + block_rows - 1, dtype=jnp.int32) - (block_rows - 1)
        distance = (own_places[0] - key_firsts)[:, None] + diagonal[None, :]
        number = bucket_levels(distance, length)
        onehot = (number[:, :, None] == bucket_ids[None, None, :]).astype(jnp.float32)
        vector = jnp.einsum("mpc,hc->mhp", onehot, table_full, precision=highest)
        band = toeplitz_band(vector, block_rows, block_rows)
        bias = jnp.transpose(band, (1, 2, 0, 3)).reshape(head_count, block_rows, key_count)
        bias = jnp.concatenate([bias, bias], axis=1)
        content_term = jnp.einsum(
            "rhe,khe->hrk", query_low, key_heads, preferred_element_type=jnp.float32
        )
        differ = (row_segments[:, None] != segs_part[None, :]).astype(jnp.float32)
        segment_term = seg_zero[:, :, None] + (seg_one - seg_zero)[:, :, None] * differ[None]
        scores = (content_term + segment_term) * 0.125 + bias
        key_index = offset + jnp.arange(key_count, dtype=jnp.int32)
        allowed = allowed_pairs(row_ranks, row_streams, row_index, ranks_part, key_index)[None]
        return (scores, differ, allowed, onehot, block_rows, pieces, key_heads, value_heads)

    def forward_step(running, portion, offset):
        running_max, running_sum, running_out = running
        scores, differ, allowed, onehot, split, pieces, key_heads, value_heads = key_scores(
            portion, offset
        )
        masked = jnp.where(allowed, scores, negative)
        new_max = jnp.maximum(running_max, jnp.max(masked, axis=2))
        weights = jnp.where(allowed, jnp.exp(masked - new_max[:, :, None]), 0.0)
        factor = jnp.exp(running_max - new_max)
        running_sum = running_sum * factor + jnp.sum(weights, axis=2)
        update = jnp.einsum(
            "hrk,khe->rhe",
            weights.astype(jnp.bfloat16),
            value_heads,
            preferred_element_type=jnp.float32,
        )
        running_out = running_out * factor.T[:, :, None] + update
        return (new_max, running_sum, running_out)

    forward_start = (
        jnp.full((head_count, row_count), negative, jnp.float32),
        jnp.zeros((head_count, row_count), jnp.float32),
        jnp.zeros((row_count, head_count, head_size), jnp.float32),
    )
    forward_state = in_blocks(
        forward_step,
        forward_start,
        (
            lax.all_gather(key_low, "ctx", axis=0, tiled=True),
            lax.all_gather(value_low, "ctx", axis=0, tiled=True),
            lax.all_gather(rank_tokens, "ctx", axis=0, tiled=True),
            lax.all_gather(own_places, "ctx", axis=0, tiled=True),
            lax.all_gather(own_segments, "ctx", axis=0, tiled=True),
        ),
    )
    running_max, running_sum, running_out = forward_state
    attended = running_out / running_sum.T[:, :, None]
    log_total = running_max + jnp.log(running_sum)
    out_low = attended.reshape(row_count, model_width).astype(jnp.bfloat16)
    attention_out = jnp.dot(out_low, weight_output, preferred_element_type=jnp.float32)
    residual = streams.astype(jnp.float32) + attention_out
    normed, first_back = jax.vjp(layer_norm, residual, gain_first, shift_first)
    normed_low = normed.astype(jnp.bfloat16)
    inner_pre = jnp.dot(normed_low, weight_inner, preferred_element_type=jnp.float32) + bias_inner
    active, gelu_back = jax.vjp(gelu_exact, inner_pre)
    active_low = active.astype(jnp.bfloat16)
    outer_out = jnp.dot(active_low, weight_outer, preferred_element_type=jnp.float32) + bias_outer
    final_norm, second_back = jax.vjp(layer_norm, normed + outer_out, gain_second, shift_second)
    squares = lax.psum(
        (
            jnp.sum(jnp.square(own_content.astype(jnp.float32))),
            jnp.sum(jnp.square(attention_out[:block_rows])),
            jnp.sum(jnp.square(residual[:block_rows])),
        ),
        ("ctx", "wsh"),
    )
    token_total = length * lax.axis_size("wsh") * model_width
    root_mean = jnp.sqrt(jnp.stack([squares[0], squares[1], squares[2]]) / token_total)
    cotangent = jnp.concatenate([content_cotangent[0], query_cotangent[0]], axis=0).astype(
        jnp.float32
    )
    back_second, final_gain_back, final_shift_back = second_back(cotangent)
    outer_back = back_second.astype(jnp.bfloat16)
    outer_weight_back = jnp.dot(active_low.T, outer_back, preferred_element_type=jnp.float32)
    outer_bias_back = jnp.sum(outer_back.astype(jnp.float32), axis=0)
    active_back = jnp.dot(outer_back, weight_outer.T, preferred_element_type=jnp.float32)
    inner_back = gelu_back(active_back)[0].astype(jnp.bfloat16)
    inner_weight_back = jnp.dot(normed_low.T, inner_back, preferred_element_type=jnp.float32)
    inner_bias_back = jnp.sum(inner_back.astype(jnp.float32), axis=0)
    normed_back = back_second + jnp.dot(
        inner_back, weight_inner.T, preferred_element_type=jnp.float32
    )
    residual_back, first_gain_back, first_shift_back = first_back(normed_back)
    attention_back = residual_back.astype(jnp.bfloat16)
    output_weight_back = jnp.dot(out_low.T, attention_back, preferred_element_type=jnp.float32)
    out_back = (
        jnp.dot(attention_back, weight_output.T, preferred_element_type=jnp.float32)
        .astype(jnp.bfloat16)
        .reshape(row_count, head_count, head_size)
    )
    row_delta = jnp.sum(out_back.astype(jnp.float32) * attended, axis=2).T

    def backward_terms(running, portion, offset):
        back_query, back_zero, back_one, back_table = running
        key_count = portion[0].shape[0]
        scores, differ, allowed, onehot, split, pieces, key_heads, value_heads = key_scores(
            portion, offset
        )
        attend_weights = jnp.where(
            allowed, jnp.exp(jnp.where(allowed, scores, 0.0) - log_total[:, :, None]), 0.0
        )
        weights_back = jnp.einsum(
            "rhe,khe->hrk", out_back, value_heads, preferred_element_type=jnp.float32
        )
        score_back = (attend_weights * (weights_back - row_delta[:, :, None])).astype(jnp.bfloat16)
        back_query = (
            back_query
            + jnp.einsum("hrk,khe->rhe", score_back, key_heads, preferred_element_type=jnp.float32)
            * 0.125
        )
        keys_term = (
            jnp.einsum("hrk,rhe->khe", score_back, query_low, preferred_element_type=jnp.float32)
            * 0.125
        )
        values_term = jnp.einsum(
            "hrk,rhe->khe",
            attend_weights.astype(jnp.bfloat16),
            out_back,
            preferred_element_type=jnp.float32,
        )
        score_wide = score_back.astype(jnp.float32)
        across = jnp.sum(score_wide * differ[None], axis=2) * 0.125
        back_one = back_one + across
        back_zero = back_zero + jnp.sum(score_wide, axis=2) * 0.125 - across
        halves = score_wide[:, :block_rows] + score_wide[:, block_rows:]
        per_piece = jnp.transpose(
            halves.reshape(head_count, block_rows, pieces, split), (2, 0, 1, 3)
        )
        diagonal_sums = band_sums(per_piece, block_rows, split)
        back_table = back_table + jnp.einsum(
            "mhp,mpc->hc", diagonal_sums, onehot, precision=highest
        )
        return (
            (back_query, back_zero, back_one, back_table),
            keys_term.reshape(key_count, model_width),
            values_term.reshape(key_count, model_width),
        )

    def backward_step(running, portion, offset):
        inner_state, keys_term, values_term = backward_terms(running[:4], portion, offset)
        back_keys = lax.dynamic_update_slice_in_dim(running[4], keys_term, offset, 0)
        back_values = lax.dynamic_update_slice_in_dim(running[5], values_term, offset, 0)
        return inner_state + (back_keys, back_values)

    attention_start = (
        jnp.zeros((row_count, head_count, head_size), jnp.float32),
        jnp.zeros((head_count, row_count), jnp.float32),
        jnp.zeros((head_count, row_count), jnp.float32),
        jnp.zeros(table_full.shape, jnp.float32),
    )
    full_start = attention_start + (
        jnp.zeros((length, model_width), jnp.float32),
        jnp.zeros((length, model_width), jnp.float32),
    )
    backward_state = in_blocks(
        backward_step,
        full_start,
        (
            lax.all_gather(key_low, "ctx", axis=0, tiled=True),
            lax.all_gather(value_low, "ctx", axis=0, tiled=True),
            lax.all_gather(rank_tokens, "ctx", axis=0, tiled=True),
            lax.all_gather(own_places, "ctx", axis=0, tiled=True),
            lax.all_gather(own_segments, "ctx", axis=0, tiled=True),
        ),
    )
    back_query, back_zero, back_one, back_table, back_keys, back_values = backward_state
    key_total, value_total = (
        lax.psum_scatter(back_keys, "ctx", scatter_dimension=0, tiled=True),
        lax.psum_scatter(back_values, "ctx", scatter_dimension=0, tiled=True),
    )
    keys_back = key_total.astype(jnp.bfloat16)
    values_back = value_total.astype(jnp.bfloat16)
    content_bias_back = jnp.sum(back_query, axis=0).reshape(model_width)
    shift_back = (
        back_zero.T[:, :, None] * embed_pair[0][None] + back_one.T[:, :, None] * embed_pair[1][None]
    )
    segment_bias_back = jnp.sum(shift_back, axis=0).reshape(model_width)
    embed_zero_back = jnp.sum(back_zero.T[:, :, None] * query_shift, axis=0).reshape(model_width)
    embed_one_back = jnp.sum(back_one.T[:, :, None] * query_shift, axis=0).reshape(model_width)
    segment_embed_back = jnp.stack([embed_zero_back, embed_one_back])
    query_back = (back_query + shift_back).reshape(row_count, model_width).astype(jnp.bfloat16)
    query_weight_back = jnp.dot(streams.T, query_back, preferred_element_type=jnp.float32)
    key_weight_back = jnp.dot(own_content.T, keys_back, preferred_element_type=jnp.float32)
    value_weight_back = jnp.dot(own_content.T, values_back, preferred_element_type=jnp.float32)
    streams_back = residual_back + jnp.dot(
        query_back, weight_query.T, preferred_element_type=jnp.float32
    )
    content_back = (
        streams_back[:block_rows]
        + jnp.dot(keys_back, weight_key.T, preferred_element_type=jnp.float32)
        + jnp.dot(values_back, weight_value.T, preferred_element_type=jnp.float32)
    )
    query_stream_back = streams_back[block_rows:]
    shard_back = (
        lax.psum_scatter(
            query_weight_back.astype(jnp.bfloat16), "wsh", scatter_dimension=0, tiled=True
        ).astype(jnp.float32),
        lax.psum_scatter(
            key_weight_back.astype(jnp.bfloat16), "wsh", scatter_dimension=0, tiled=True
        ).astype(jnp.float32),
        lax.psum_scatter(
            value_weight_back.astype(jnp.bfloat16), "wsh", scatter_dimension=0, tiled=True
        ).astype(jnp.float32),
        lax.psum_scatter(
            output_weight_back.astype(jnp.bfloat16), "wsh", scatter_dimension=0, tiled=True
        ).astype(jnp.float32),
        lax.psum_scatter(
            content_bias_back.astype(jnp.bfloat16), "wsh", scatter_dimension=0, tiled=True
        ).astype(jnp.float32),
        lax.psum_scatter(
            segment_bias_back.astype(jnp.bfloat16), "wsh", scatter_dimension=0, tiled=True
        ).astype(jnp.float32),
        lax.psum_scatter(
            segment_embed_back.astype(jnp.bfloat16), "wsh", scatter_dimension=1, tiled=True
        ).astype(jnp.float32),
        lax.psum_scatter(
            back_table.astype(jnp.bfloat16), "wsh", scatter_dimension=0, tiled=True
        ).astype(jnp.float32),
        lax.psum_scatter(
            first_gain_back.astype(jnp.bfloat16), "wsh", scatter_dimension=0, tiled=True
        ).astype(jnp.float32),
        lax.psum_scatter(
            first_shift_back.astype(jnp.bfloat16), "wsh", scatter_dimension=0, tiled=True
        ).astype(jnp.float32),
        lax.psum_scatter(
            inner_weight_back.astype(jnp.bfloat16), "wsh", scatter_dimension=0, tiled=True
        ).astype(jnp.float32),
        lax.psum_scatter(
            inner_bias_back.astype(jnp.bfloat16), "wsh", scatter_dimension=0, tiled=True
        ).astype(jnp.float32),
        lax.psum_scatter(
            outer_weight_back.astype(jnp.bfloat16), "wsh", scatter_dimension=0, tiled=True
        ).astype(jnp.float32),
        lax.psum_scatter(
            outer_bias_back.astype(jnp.bfloat16), "wsh", scatter_dimension=0, tiled=True
        ).astype(jnp.float32),
        lax.psum_scatter(
            final_gain_back.astype(jnp.bfloat16), "wsh", scatter_dimension=0, tiled=True
        ).astype(jnp.float32),
        lax.psum_scatter(
            final_shift_back.astype(jnp.bfloat16), "wsh", scatter_dimension=0, tiled=True
        ).astype(jnp.float32),
    )
    totals = lax.psum(
        (
            shard_back[0],
            shard_back[1],
            shard_back[2],
            shard_back[3],
            shard_back[4],
            shard_back[5],
            shard_back[6],
            shard_back[7],
            shard_back[8],
            shard_back[9],
            shard_back[10],
            shard_back[11],
            shard_back[12],
            shard_back[13],
            shard_back[14],
            shard_back[15],
        ),
        "ctx",
    )
    return (
        final_norm[:block_rows].astype(jnp.bfloat16)[None],
        final_norm[block_rows:].astype(jnp.bfloat16)[None],
        content_back[None],
        query_stream_back[None],
        totals[0],
        totals[1],
        totals[2],
        totals[3],
        totals[4],
        totals[5],
        totals[6],
        totals[7],
        totals[8],
        totals[9],
        totals[10],
        totals[11],
        totals[12],
        totals[13],
        totals[14],
        totals[15],
        root_mean,
    )


def solution(mesh):
    placed = (
        P("wsh", "ctx", None),
        P("wsh", "ctx", None),
        P("wsh", "ctx"),
        P("wsh", "ctx"),
        P("wsh", "ctx"),
        P("wsh", None),
        P("wsh", None),
        P("wsh", None),
        P("wsh", None),
        P("wsh"),
        P("wsh"),
        P(None, "wsh"),
        P("wsh", None),
        P("wsh"),
        P("wsh"),
        P("wsh", None),
        P("wsh"),
        P("wsh", None),
        P("wsh"),
        P("wsh"),
        P("wsh"),
        P("wsh", "ctx", None),
        P("wsh", "ctx", None),
    )
    return jax.shard_map(
        body,
        mesh=mesh,
        in_specs=placed,
        out_specs=(
            P("wsh", "ctx", None),
            P("wsh", "ctx", None),
            P("wsh", "ctx", None),
            P("wsh", "ctx", None),
            P("wsh", None),
            P("wsh", None),
            P("wsh", None),
            P("wsh", None),
            P("wsh"),
            P("wsh"),
            P(None, "wsh"),
            P("wsh", None),
            P("wsh"),
            P("wsh"),
            P("wsh", None),
            P("wsh"),
            P("wsh", None),
            P("wsh"),
            P("wsh"),
            P("wsh"),
            P(),
        ),
        check_vma=False,
    )
```

profile of v0, /device:TPU:1, one launch (start us, length us, event | category | flops | bytes accessed | tf_op | source)
XLA Modules:
  0.0 1594.1 jit_solution(3261787795144182414)
XLA Ops:
  9.5 25.0 %all-gather.27.cloned.1.call-done = bf16[768,768]{1,0:T(8,128)(2,1)} async-done(((bf16[384,768]{1,0:T(8,128)(2,1)}), bf16[768,768]{1,0:T(8,128)(2,1)}) %all-gather.27.cloned.1.call-update) | async-done | bytes 1179664 | tf_op jit(solution)/shard_map/all_gather | solution.py:109
  36.9 21.9 %all-gather.21.cloned.1.call-done = bf16[768,768]{1,0:T(8,128)(2,1)} async-done(((bf16[384,768]{1,0:T(8,128)(2,1)}), bf16[768,768]{1,0:T(8,128)(2,1)}) %all-gather.21.cloned.1.call-update) | async-done | bytes 1179664 | tf_op jit(solution)/shard_map/all_gather | solution.py:108
  102.1 31.6 %all-gather.2 = s32[16,1,128]{2,1,0:T(1,128)S(1)} all-gather(s32[1,1,128]{2,1,0:T(1,128)S(1)} %broadcast.1153), channel_id=1, replica_groups=mesh['ctx'=16,'wsh'=2] {'ctx'}, dimensions={0}, use_global_device_ids=true | all-gather | bytes 8704 | tf_op jit(solution)/shard_map/all_gather | solution.py:227
  135.0 17.3 %all-gather = s32[1,2048]{1,0:T(1,128)S(1)} all-gather(s32[1,128]{1,0:T(1,128)S(1)} %copy-done.94), channel_id=2, replica_groups=mesh['ctx'=16,'wsh'=2] {'ctx'}, dimensions={1}, use_global_device_ids=true | all-gather | bytes 8704 | tf_op jit(solution)/shard_map/all_gather | solution.py:229
  152.9 18.9 %all-gather.1 = s32[1,2048]{1,0:T(1,128)S(1)} all-gather(s32[1,128]{1,0:T(1,128)} %param.31), channel_id=3, replica_groups=mesh['ctx'=16,'wsh'=2] {'ctx'}, dimensions={1}, use_global_device_ids=true | all-gather | bytes 8704 | tf_op jit(solution)/shard_map/all_gather | solution.py:228
  183.9 184.8 %while.40 = (s32[]{:T(128)}, f32[12,256]{1,0:T(8,128)S(1)}, f32[12,256]{1,0:T(8,128)S(1)}, f32[256,12,64]{0,2,1:T(8,128)}, s32[2,1024]{1,0:T(2,128)S(1)}, /*inde...) while((s32[]{:T(128)}, f32[12,256]{1,0:T(8,128)S(1)}, ...), condition=%wide.region_5.6_spmd.clone, body=%wide.region_2.5_spmd.clone.sunk | while | flops 861490304 | bytes 179100464 | solution.py:72
  228.0 22.0 %reshape.943 = f32[8,12,128,254]{3,2,0,1:T(8,128)} reshape(f32[8,12,32512]{2,0,1:T(8,128)} %slice.157) | data formatting | bytes 24969216 | tf_op jit(solution)/shard_map/while/body/eval_jaxpr/reshape | solution.py:41
  319.3 22.0 %reshape.943 = f32[8,12,128,254]{3,2,0,1:T(8,128)} reshape(f32[8,12,32512]{2,0,1:T(8,128)} %slice.157) | data formatting | bytes 24969216 | tf_op jit(solution)/shard_map/while/body/eval_jaxpr/reshape | solution.py:41
  414.2 453.5 %while.41 = (s32[]{:T(128)}, f32[256,12,64]{0,2,1:T(8,128)}, f32[12,256]{1,0:T(8,128)}, f32[12,256]{1,0:T(8,128)}, f32[12,33]{1,0:T(8,128)}, /*index=5*/f32[2048...) while((s32[]{:T(128)}, f32[256,12,64]{0,2,1:T(8,128)}, ...), condition=%wide.region_19.20_spmd.clone, body=%wide.region_15.19_spmd.clone.sunk | while | flops 2097284608 | bytes 478649536 | solution.py:72
  467.8 22.1 %reshape.944 = f32[8,12,128,254]{3,2,0,1:T(8,128)} reshape(f32[8,12,32512]{2,0,1:T(8,128)} %slice.163) | data formatting | bytes 24969216 | tf_op jit(solution)/shard_map/while/body/eval_jaxpr/reshape | solution.py:41
  530.7 15.6 dynamic_update_slice.17
  614.3 16.6 %reshape.946 = f32[8,12,129,255]{3,2,0,1:T(8,128)} reshape(f32[8,12,32895]{2,0,1:T(8,128)} %pad.85) | data formatting | bytes 25263360 | tf_op jit(solution)/shard_map/while/body/eval_jaxpr/reshape | solution.py:50
  694.8 22.1 %reshape.944 = f32[8,12,128,254]{3,2,0,1:T(8,128)} reshape(f32[8,12,32512]{2,0,1:T(8,128)} %slice.163) | data formatting | bytes 24969216 | tf_op jit(solution)/shard_map/while/body/eval_jaxpr/reshape | solution.py:41
  839.5 16.6 %reshape.946 = f32[8,12,129,255]{3,2,0,1:T(8,128)} reshape(f32[8,12,32895]{2,0,1:T(8,128)} %pad.85) | data formatting | bytes 25263360 | tf_op jit(solution)/shard_map/while/body/eval_jaxpr/reshape | solution.py:50
  890.0 61.0 %reduce-scatter.18.cloned.1.call-done = f32[128,768]{0,1:T(8,128)} async-done(((f32[2048,768]{0,1:T(8,128)}), f32[128,768]{0,1:T(8,128)}) %reduce-scatter.18.cloned.1.call-update) | async-done | bytes 393232 | tf_op jit(solution)/shard_map/reduce_scatter | solution.py:355
  960.7 41.7 %all-reduce.11 = (f32[1]{0:T(128)}, f32[1]{0:T(128)}, f32[1]{0:T(128)}) all-reduce(f32[1]{0:T(128)} %bitcast.33, f32[1]{0:T(128)} %bitcast.32, f32[1]{0:T(128)} %bitcast.31), channel_id=1, replica_groups=mesh['ctx'=16,'wsh'=2] {'ctx','wsh'}, use_global_device_ids=true, to_apply=%region_70.71 | all-reduce | flops 3 | bytes 24 | tf_op jit(solution)/shard_map/psum | solution.py:245
  1008.9 31.4 %reduce-scatter.16.cloned.1.call-done = f32[128,768]{0,1:T(8,128)} async-done(((f32[2048,768]{0,1:T(8,128)}), f32[128,768]{0,1:T(8,128)}) %reduce-scatter.16.cloned.1.call-update) | async-done | bytes 393232 | tf_op jit(solution)/shard_map/reduce_scatter | solution.py:354
  1061.5 16.3 %reduce-scatter.22.cloned.1.call-done = bf16[384,768]{1,0:T(8,128)(2,1)} async-done(((bf16[768,768]{1,0:T(8,128)(2,1)}), bf16[384,768]{1,0:T(8,128)(2,1)}) %reduce-scatter.22.cloned.1.call-update) | async-done | bytes 589840 | tf_op jit(solution)/shard_map/reduce_scatter | solution.py:390
  1077.8 24.7 %reduce-scatter.20.cloned.1.call-done = bf16[384,768]{1,0:T(8,128)(2,1)} async-done(((bf16[768,768]{1,0:T(8,128)(2,1)}), bf16[384,768]{1,0:T(8,128)(2,1)}) %reduce-scatter.20.cloned.1.call-update) | async-done | bytes 589840 | tf_op jit(solution)/shard_map/reduce_scatter | solution.py:381
  1102.5 62.8 %reduce-scatter.24.cloned.1.call-done = bf16[384,3072]{1,0:T(8,128)(2,1)} async-done(((bf16[768,3072]{1,0:T(8,128)(2,1)}), bf16[384,3072]{1,0:T(8,128)(2,1)}) %reduce-scatter.24.cloned.1.call-update) | async-done | bytes 2359312 | tf_op jit(solution)/shard_map/reduce_scatter | solution.py:411
  1165.3 62.9 %reduce-scatter.26.cloned.1.call-done = bf16[1536,768]{1,0:T(8,128)(2,1)} async-done(((bf16[3072,768]{1,0:T(8,128)(2,1)}), bf16[1536,768]{1,0:T(8,128)(2,1)}) %reduce-scatter.26.cloned.1.call-update) | async-done | bytes 2359312 | tf_op jit(solution)/shard_map/reduce_scatter | solution.py:417
  1232.3 20.3 %reduce-scatter.30.cloned.1.call-done = bf16[384,768]{1,0:T(8,128)(2,1)} async-done(((bf16[768,768]{1,0:T(8,128)(2,1)}), bf16[384,768]{1,0:T(8,128)(2,1)}) %reduce-scatter.30.cloned.1.call-update) | async-done | bytes 589840
  1254.0 23.2 %reduce-scatter.28.cloned.1.call-done = bf16[384,768]{1,0:T(8,128)(2,1)} async-done(((bf16[768,768]{1,0:T(8,128)(2,1)}), bf16[384,768]{1,0:T(8,128)(2,1)}) %reduce-scatter.28.cloned.1.call-update) | async-done | bytes 589840
  1278.5 304.7 %all-reduce.15 = (f32[384,768]{1,0:T(8,128)}, f32[384,768]{0,1:T(8,128)}, f32[384,768]{0,1:T(8,128)}, f32[384,768]{1,0:T(8,128)}, f32[384]{0:T(512)}, /*index=5*...) all-reduce(bf16[384,768]{1,0:T(8,128)(2,1)} %reduce-scatter.20.clon, ...), channel_id=1, replica_groups=mesh['ctx'=16,'wsh'=2] {'ctx'}, use_global_device_ids=true, to_apply=%region_23.24 | all-reduce | flops 3544134 | bytes 21273648 | tf_op jit(solution)/shard_map/psum | solution.py:430
  (566 shorter events, 669.8 us)
Async XLA Ops:
  7.2 27.3 %all-gather.27.cloned.1.call-start = ((), (), s32[]{:S(2)}) async-start(), calls=%async_computation.12 | async-start | bytes 1769472 | tf_op jit(solution)/shard_map/all_gather | solution.py:109
  7.9 50.9 %all-gather.21.cloned.1.call-start = ((), (), s32[]{:S(2)}) async-start(), calls=%async_computation.9 | async-start | bytes 1769472 | tf_op jit(solution)/shard_map/all_gather | solution.py:108
  8.7 163.9 %all-gather.25.cloned.1.call-start = ((), (), s32[]{:S(2)}) async-start(), calls=%async_computation.11 | async-start | bytes 1769472 | tf_op jit(solution)/shard_map/all_gather | solution.py:107
  9.4 166.6 %all-gather.29.cloned.1.call-start = ((), (), s32[]{:S(2)}) async-start(), calls=%async_computation.13 | async-start | bytes 3342336 | tf_op jit(solution)/shard_map/all_gather | solution.py:226
  36.9 142.3 %all-gather.23.cloned.1.call-start = ((), (), s32[]{:S(2)}) async-start(), calls=%async_computation.10 | async-start | bytes 3342336 | tf_op jit(solution)/shard_map/all_gather | solution.py:225
  61.2 309.4 %all-gather.31.cloned.1.call-start = ((), (), s32[]{:S(2)}) async-start(), calls=%async_computation.14 | async-start | bytes 1769472 | tf_op jit(solution)/shard_map/all_gather | solution.py:110
  61.8 314.0 %all-gather.33.cloned.1.call-start = ((), (), s32[]{:S(2)}) async-start(), calls=%async_computation.15 | async-start | bytes 7077888 | tf_op jit(solution)/shard_map/all_gather | solution.py:117
  62.6 326.2 %all-gather.35.cloned.1.call-start = ((), (), s32[]{:S(2)}) async-start(), calls=%async_computation.16 | async-start | bytes 7077888 | tf_op jit(solution)/shard_map/all_gather | solution.py:119
  63.3 887.7 %reduce-scatter.18.cloned.1.call-start = ((), (), s32[]{:S(2)}) async-start(), calls=%async_computation.18 | async-start | bytes 6684672 | tf_op jit(solution)/shard_map/reduce_scatter | solution.py:355
  867.8 172.6 %reduce-scatter.16.cloned.1.call-start = ((), (), s32[]{:S(2)}) async-start(), calls=%async_computation.17 | async-start | bytes 6684672 | tf_op jit(solution)/shard_map/reduce_scatter | solution.py:354
  868.4 191.6 %reduce-scatter.32.cloned.1.call-start = ((), (), s32[]{:S(2)}) async-start(), calls=%async_computation.25 | async-start | bytes 294912
  873.6 204.2 %reduce-scatter.22.cloned.1.call-start = ((), (), s32[]{:S(2)}) async-start(), calls=%async_computation.20 | async-start | bytes 1769472 | tf_op jit(solution)/shard_map/reduce_scatter | solution.py:390
  875.3 227.2 %reduce-scatter.20.cloned.1.call-start = ((), (), s32[]{:S(2)}) async-start(), calls=%async_computation.19 | async-start | bytes 1769472 | tf_op jit(solution)/shard_map/reduce_scatter | solution.py:381
  878.2 287.1 %reduce-scatter.24.cloned.1.call-start = ((), (), s32[]{:S(2)}) async-start(), calls=%async_computation.21 | async-start | bytes 7077888 | tf_op jit(solution)/shard_map/reduce_scatter | solution.py:411
  883.7 344.5 %reduce-scatter.26.cloned.1.call-start = ((), (), s32[]{:S(2)}) async-start(), calls=%async_computation.22 | async-start | bytes 7077888 | tf_op jit(solution)/shard_map/reduce_scatter | solution.py:417
  889.9 112.7 %copy-start.86 = (bf16[768]{0:T(1024)(128)(2,1)S(1)}, bf16[768]{0:T(1024)(128)(2,1)}, u32[]{:S(2)}) copy-start(bf16[768]{0:T(1024)(128)(2,1)} %get-tuple-element.980) | copy-start | bytes 4612
  889.9 112.7 %copy-start.87 = (bf16[768]{0:T(1024)(128)(2,1)S(1)}, bf16[768]{0:T(1024)(128)(2,1)}, u32[]{:S(2)}) copy-start(bf16[768]{0:T(1024)(128)(2,1)} %get-tuple-element.1103) | copy-start | bytes 4612
  889.9 112.7 %copy-start.89 = (bf16[3072]{0:T(1024)(128)(2,1)S(1)}, bf16[3072]{0:T(1024)(128)(2,1)}, u32[]{:S(2)}) copy-start(bf16[3072]{0:T(1024)(128)(2,1)} %get-tuple-element.1105) | copy-start | bytes 18436
  889.9 112.7 %copy-start.92 = (bf16[768]{0:T(1024)(128)(2,1)S(1)}, bf16[768]{0:T(1024)(128)(2,1)}, u32[]{:S(2)}) copy-start(bf16[768]{0:T(1024)(128)(2,1)} %get-tuple-element.978) | copy-start | bytes 4612
  889.9 362.7 %reduce-scatter.30.cloned.1.call-start = ((), (), s32[]{:S(2)}) async-start(), calls=%async_computation.24 | async-start | bytes 1769472
  955.9 321.3 %reduce-scatter.28.cloned.1.call-start = ((), (), s32[]{:S(2)}) async-start(), calls=%async_computation.23 | async-start | bytes 1769472
  1043.2 184.9 %copy-start.18 = (bf16[768,768]{1,0:T(8,128)(2,1)S(1)}, bf16[768,768]{1,0:T(8,128)(2,1)}, u32[]{:S(2)}) copy-start(bf16[768,768]{1,0:T(8,128)(2,1)} %all-gather.21.cloned.1.call-done) | copy-start | bytes 3538948
  1056.4 173.4 %copy-start.17 = (bf16[768,768]{1,0:T(8,128)(2,1)S(1)}, bf16[768,768]{1,0:T(8,128)(2,1)}, u32[]{:S(2)}) copy-start(bf16[768,768]{1,0:T(8,128)(2,1)} %all-gather.27.cloned.1.call-done) | copy-start | bytes 3538948
  1061.5 217.0 %copy-start.88 = (f32[384]{0:T(512)S(1)}, f32[384]{0:T(512)}, u32[]{:S(2)}) copy-start(f32[384]{0:T(512)} %dynamic-slice_convert_fusion.8) | copy-start | bytes 4612
  (121 other events, 1624.8 us)
Sparse Core Ops, SparseCore 0:
  9.6 24.8 all-gather.26
  36.0 22.7 all-gather.20
  60.4 22.8 all-gather.24
  86.0 45.6 all-gather.28
  134.4 44.2 all-gather.22
  180.1 21.1 all-gather.30
  202.9 62.6 all-gather.32
  267.1 62.6 all-gather.34
  867.9 83.0 reduce-scatter.17
  955.3 84.9 reduce-scatter.15
  1042.6 10.8 reduce-scatter.31
  1056.1 21.6 reduce-scatter.21
  1080.7 21.7 reduce-scatter.19
  1105.3 59.9 reduce-scatter.23
  1168.1 59.9 reduce-scatter.25
  1230.8 21.7 reduce-scatter.29
  1255.4 21.7 reduce-scatter.27
where the time goes:
time: 1600 us; the launch traced here: 1590 us
  local copies, waits for them, and re-layouts  543 us (34%)
  blocking collectives  454 us (28%)
  waiting for transfers between devices  354 us (22%)
  matrix products  135 us (8%)
  other arithmetic  84.2 us (5%)
  between operations  18 us (1%)
    psum x1, blocking collectives, body(): lax.psum((shard_back[0], shard_back[1], shard_back[2], shard_back[3], sha...  305 us
    reshape x4, local copies, waits for them, and re-layouts, toeplitz_band(): return flat.reshape(vector.shape[:-1] + (rows, width - 1))[..., :cols]  88.2 us
    another operation x8, local copies, waits for them, and re-layouts, toeplitz_band(): tiled = jnp.tile(flipped, (1,) * (vector.ndim - 1) + (rows + 1,))  84.7 us
    reduce_scatter x1, waiting for transfers between devices, body(): lax.psum_scatter(outer_weight_back.astype(jnp.bfloat16), 'wsh', scatter_d...  62.9 us
    reduce_scatter x1, waiting for transfers between devices, body(): lax.psum_scatter(inner_weight_back.astype(jnp.bfloat16), 'wsh', scatter_d...  62.8 us
    reduce_scatter x1, waiting for transfers between devices, body(): lax.psum_scatter(back_values, 'ctx', scatter_dimension=0, tiled=True)  61 us
    transpose x8, local copies, waits for them, and re-layouts, key_scores(): jnp.transpose(band, (1, 2, 0, 3)).reshape(head_count, block_rows, key_count)  51.7 us
    slice x4, local copies, waits for them, and re-layouts, toeplitz_band(): lax.slice_in_dim(tiled, start, start + rows * (width - 1), axis=vector.nd...  49.8 us
  transfers between devices with their start and end apart: 17, of which 10 were waited for; matrix products, arithmetic and copies ran while one was open for 17% of the time, Pallas kernels for 0%

commit v1 on v0

v1 whole, which is shorter than its diff:
```python
import functools

import jax
import jax.numpy as jnp
from jax import lax
from jax.experimental import pallas as pl
from jax.experimental.pallas import tpu as pltpu
from jax.sharding import PartitionSpec as P

negative = -1e30
epsilon = 1e-05
bucket_steps = 16
key_tile = 256
lanes = 128
highest = lax.Precision.HIGHEST
f32 = jnp.float32
bf16 = jnp.bfloat16


def layer_norm(values, gain_row, shift_row):
    centred = values - jnp.mean(values, axis=-1, keepdims=True)
    spread = jnp.mean(centred * centred, axis=-1, keepdims=True)
    return centred * lax.rsqrt(spread + epsilon) * gain_row + shift_row


def gelu_exact(values):
    return jax.nn.gelu(values, approximate=False)


def bucket_levels(distance, length):
    result = jnp.full(distance.shape, bucket_steps, jnp.int32)
    for level_index in range(bucket_steps):
        bound_value = 1 + level_index * level_index * length // (bucket_steps * bucket_steps)
        result = (
            result
            + (distance >= bound_value).astype(jnp.int32)
            - (distance <= -bound_value).astype(jnp.int32)
        )
    return result


def dot(left, right):
    return jnp.dot(left, right, preferred_element_type=f32)


def dot_nt(left, right):
    return lax.dot_general(left, right, (((1,), (1,)), ((), ())), preferred_element_type=f32)


def dot_tn(left, right):
    return lax.dot_general(left, right, (((0,), (0,)), ((), ())), preferred_element_type=f32)


def partner(value, bit):
    count = lax.axis_size("ctx")
    return lax.ppermute(value, "ctx", [(place, place ^ bit) for place in range(count)])


def across(value):
    return lax.ppermute(value, "wsh", [(0, 1), (1, 0)])


def bits_of(count):
    result = []
    bit = 1
    while bit < count:
        result.append(bit)
        bit *= 2
    return result


def block_order(count):
    order = [0]
    for bit in reversed(bits_of(count)):
        order = order + [place | bit for place in order]
    return order


def gather_blocks(own):
    count = lax.axis_size("ctx")
    bits = bits_of(count)
    held = {0: own}
    top = bits[-2:]
    for place in (top[0], top[1], top[0] | top[1]):
        held[place] = partner(own, place)
    for bit in reversed(bits[:-2]):
        for place in list(held):
            held[place | bit] = partner(held[place], bit)
    return [held[place] for place in block_order(count)]


def scatter_blocks(total):
    count = lax.axis_size("ctx")
    for bit in bits_of(count):
        half = total.shape[0] // 2
        received = partner(total[half:].astype(bf16), bit)
        total = total[:half].astype(f32) + received.astype(f32)
    return total


def gather_shard(shard):
    core = lax.axis_index("ctx") % 2
    side = lax.axis_index("wsh")
    rows = shard.shape[0]
    half = rows // 2
    mine = lax.dynamic_slice_in_dim(shard, core * half, half, 0)
    got = across(mine)
    rest = partner(got, 1)
    whole = jnp.zeros((2 * rows,) + shard.shape[1:], shard.dtype)
    base = (1 - side) * rows
    whole = lax.dynamic_update_slice_in_dim(whole, shard, side * rows, 0)
    whole = lax.dynamic_update_slice_in_dim(whole, got, base + core * half, 0)
    return lax.dynamic_update_slice_in_dim(whole, rest, base + (1 - core) * half, 0)


def halve(value, bit, dim):
    size = value.shape[dim] // 2
    kept = lax.dynamic_slice_in_dim(value, bit * size, size, dim)
    sent = lax.dynamic_slice_in_dim(value, (1 - bit) * size, size, dim)
    return kept, sent


def join(mine, other, bit, dim):
    return jnp.where(
        bit == 0,
        jnp.concatenate([mine, other], axis=dim),
        jnp.concatenate([other, mine], axis=dim),
    )


def added(kept, received):
    return (kept.astype(f32) + received.astype(f32)).astype(bf16)


def reduce_gradient(gradient):
    index = lax.axis_index("ctx")
    side = lax.axis_index("wsh")
    count = lax.axis_size("ctx")
    value = gradient
    kept, sent = halve(value, index % 2, 1)
    value = added(kept, partner(sent, 1))
    kept, sent = halve(value, side, 0)
    value = added(kept, across(sent))
    taken = []
    for bit in bits_of(count)[1:]:
        own_bit = (index // bit) % 2
        if (value.shape[0] // 2) % 16 == 0:
            dim = 0
        elif (value.shape[1] // 2) % 128 == 0:
            dim = 1
        else:
            dim = -1
        if dim < 0:
            value = added(value, partner(value, bit))
        else:
            kept, sent = halve(value, own_bit, dim)
            value = added(kept, partner(sent, bit))
        taken.append((bit, own_bit, dim))
    for bit, own_bit, dim in reversed(taken):
        if dim >= 0:
            value = join(value, partner(value, bit), own_bit, dim)
    value = join(value, partner(value, 1), index % 2, 1)
    return value.astype(f32)


def sum_everywhere(value):
    count = lax.axis_size("ctx")
    value = value + across(value)
    for bit in bits_of(count):
        value = value + partner(value, bit)
    return value


def stream_bias(table_ref, head, block):
    spread = jnp.broadcast_to(table_ref[head, pl.ds(block, 1), :], (lanes, 2 * lanes))
    return pltpu.roll(spread, 0, 1, stride=1, stride_axis=0)[:, :lanes]


def tile_bias(table_ref, block):
    parts = []
    for piece in range(key_tile // lanes):
        first = stream_bias(table_ref, 0, block + piece)
        second = stream_bias(table_ref, 1, block + piece)
        parts.append(jnp.concatenate([first, first, second, second], axis=1))
    return jnp.concatenate(parts, axis=0)


def own_mask():
    row = lax.broadcasted_iota(jnp.int32, (key_tile, 4 * lanes), 0)
    column = lax.broadcasted_iota(jnp.int32, (key_tile, 4 * lanes), 1)
    stream = (column // lanes) % 2
    return jnp.where((stream == 1) & (row == column % lanes), negative, 0.0)


def forward_kernel(
    query_ref,
    content_bias_ref,
    segment_bias_ref,
    embed_ref,
    row_code_ref,
    key_code_ref,
    key_ref,
    value_ref,
    table_ref,
    out_ref,
    log_ref,
    stack_ref,
    score_ref,
):
    rows = query_ref.shape[0]
    tiles = key_ref.shape[0] // key_tile
    lane = lax.broadcasted_iota(jnp.int32, (rows, lanes), 1)
    first = lane < lanes // 2
    query = query_ref[...]
    low = (query + content_bias_ref[...]).astype(bf16).astype(f32) * 0.125
    shifted = query + segment_bias_ref[...]
    zero_term = shifted * embed_ref[0:1, :]
    one_term = shifted * embed_ref[1:2, :]
    code = row_code_ref[...]
    for head in range(2):
        own = first if head == 0 else jnp.logical_not(first)
        zero_sum = jnp.sum(jnp.where(own, zero_term, 0.0), axis=1, keepdims=True) * 0.125
        one_sum = jnp.sum(jnp.where(own, one_term, 0.0), axis=1, keepdims=True) * 0.125
        step = zero_sum - one_sum
        step_high = step.astype(bf16).astype(f32)
        step_low = step - step_high
        one_high = one_sum.astype(bf16).astype(f32)
        one_low = one_sum - one_high
        extra = jnp.where(
            lane < 4,
            step_high,
            jnp.where(lane < 8, step_low, jnp.where(lane == 8, one_high, one_low)),
        )
        stack_ref[0, pl.ds(head * rows, rows), 0:lanes] = jnp.where(own, low, 0.0).astype(bf16)
        stack_ref[0, pl.ds(head * rows, rows), lanes : 2 * lanes] = (extra * code).astype(bf16)
    stack = stack_ref[0]

    def scores(tile, top):
        start = pl.multiple_of(tile * key_tile, key_tile)
        keys = jnp.concatenate(
            [key_ref[pl.ds(start, key_tile), :], key_code_ref[pl.ds(start, key_tile), :]], axis=1
        )
        score = dot_nt(keys, stack) + tile_bias(table_ref, tile * (key_tile // lanes))
        if isinstance(tile, int) and tile == 0:
            score = score + own_mask()
        score_ref[pl.ds(start, key_tile), :] = score
        return jnp.maximum(top, jnp.max(score.reshape(key_tile // 8, 8, 4 * lanes), axis=0))

    top = jnp.full((8, 4 * lanes), negative, f32)
    top = scores(0, top)
    top = lax.fori_loop(1, tiles, scores, top, unroll=min(7, tiles - 1))
    peak = jnp.max(top, axis=0, keepdims=True)

    def gathered(tile, running):
        total, mixed = running
        start = pl.multiple_of(tile * key_tile, key_tile)
        weight = jnp.exp(score_ref[pl.ds(start, key_tile), :] - peak)
        total = total + jnp.sum(weight.reshape(key_tile // 8, 8, 4 * lanes), axis=0)
        mixed = mixed + dot_tn(value_ref[pl.ds(start, key_tile), :], weight.astype(bf16))
        return total, mixed

    total, mixed = lax.fori_loop(
        0,
        tiles,
        gathered,
        (jnp.zeros((8, 4 * lanes), f32), jnp.zeros((lanes, 4 * lanes), f32)),
        unroll=min(8, tiles),
    )
    total = jnp.sum(total, axis=0, keepdims=True)
    mixed = mixed / total
    half = lanes // 2
    joined = jnp.concatenate([mixed[:half, :rows], mixed[half:, rows:]], axis=0)
    out_ref[...] = joined.T
    log_ref[0] = peak + jnp.log(total)


def diagonal_sums(square):
    lane = lax.broadcasted_iota(jnp.int32, (8, lanes), 1)
    near = square[0:8]
    far = jnp.zeros((8, lanes), f32)
    for group in range(1, lanes // 8):
        turned = pltpu.roll(square[8 * group : 8 * group + 8], lanes - 8 * group, 1)
        inside = lane < lanes - 8 * group
        near = near + jnp.where(inside, turned, 0.0)
        far = far + jnp.where(inside, 0.0, turned)
    both = jnp.concatenate([near, far], axis=1)
    row = lax.broadcasted_iota(jnp.int32, (8, 2 * lanes), 0)
    for bit in (1, 2, 4):
        both = jnp.where((row // bit) % 2 == 1, pltpu.roll(both, 2 * lanes - bit, 1), both)
    return jnp.sum(both, axis=0, keepdims=True)


def backward_kernel(
    stack_ref,
    query_ref,
    segment_bias_ref,
    embed_ref,
    row_code_ref,
    key_code_ref,
    key_ref,
    value_ref,
    table_ref,
    out_back_ref,
    attended_ref,
    log_ref,
    query_back_ref,
    key_back_ref,
    value_back_ref,
    diagonal_ref,
    small_ref,
):
    rows = query_ref.shape[0]
    tiles = key_ref.shape[0] // key_tile
    half = lanes // 2
    lane = lax.broadcasted_iota(jnp.int32, (rows, lanes), 1)
    first = lane < half
    out_back = out_back_ref[...]
    product = (out_back.astype(f32) * attended_ref[...]).T
    delta = jnp.concatenate(
        [
            jnp.sum(product[:half], axis=0, keepdims=True),
            jnp.sum(product[half:], axis=0, keepdims=True),
        ],
        axis=1,
    )
    zeros = jnp.zeros_like(out_back)
    back_stack = jnp.concatenate(
        [jnp.where(first, out_back, zeros), jnp.where(first, zeros, out_back)], axis=0
    )
    stack = stack_ref[0]
    query_stack = stack[:, :lanes]
    log_row = log_ref[0]

    def step(tile, running):
        start = pl.multiple_of(tile * key_tile, key_tile)
        block = tile * (key_tile // lanes)
        keys = jnp.concatenate(
            [key_ref[pl.ds(start, key_tile), :], key_code_ref[pl.ds(start, key_tile), :]], axis=1
        )
        score = dot_nt(keys, stack) + tile_bias(table_ref, block)
        if isinstance(tile, int) and tile == 0:
            score = score + own_mask()
        weight = jnp.exp(score - log_row)
        weight_back = dot_nt(value_ref[pl.ds(start, key_tile), :], back_stack)
        score_back = weight * (weight_back - delta)
        score_low = score_back.astype(bf16)
        value_back_ref[pl.ds(start, key_tile), :] = dot(weight.astype(bf16), back_stack).astype(
            bf16
        )
        key_back_ref[pl.ds(start, key_tile), :] = dot(score_low, query_stack).astype(bf16)
        for head in range(2):
            for piece in range(key_tile // lanes):
                part = score_back[
                    piece * lanes : (piece + 1) * lanes, head * rows : (head + 1) * rows
                ]
                square = part[:, :lanes] + part[:, lanes:]
                diagonal_ref[head, pl.ds(block + piece, 1), :] = diagonal_sums(square)
        return running + dot_tn(keys, score_low)

    running = step(0, jnp.zeros((2 * lanes, 2 * rows), f32))
    running = lax.fori_loop(1, tiles, step, running, unroll=min(7, tiles - 1))
    joined = jnp.concatenate([running[:half, :rows], running[half:lanes, rows:]], axis=0).T * 0.125
    shifted = query_ref[...] + segment_bias_ref[...]
    code = row_code_ref[...]
    zero_columns = []
    one_columns = []
    for head in range(2):
        part = running[lanes:, head * rows : (head + 1) * rows].T * 0.125
        same = jnp.sum(jnp.where(lane < 4, part * code, 0.0), axis=1, keepdims=True)
        total = jnp.sum(jnp.where(lane == 8, part, 0.0), axis=1, keepdims=True)
        zero_columns.append(same)
        one_columns.append(total - same)
    zero_back = jnp.where(first, zero_columns[0], zero_columns[1])
    one_back = jnp.where(first, one_columns[0], one_columns[1])
    shift_back = zero_back * embed_ref[0:1, :] + one_back * embed_ref[1:2, :]
    query_back_ref[...] = (joined + shift_back).astype(bf16)
    small_ref[0:1, :] = jnp.sum(joined, axis=0, keepdims=True)
    small_ref[1:2, :] = jnp.sum(shift_back, axis=0, keepdims=True)
    small_ref[2:3, :] = jnp.sum(zero_back * shifted, axis=0, keepdims=True)
    small_ref[3:4, :] = jnp.sum(one_back * shifted, axis=0, keepdims=True)
    small_ref[4:8, :] = jnp.zeros((4, lanes), f32)


def attention_specs(rows, keys, blocks):
    column = lambda pair: (0, pair)
    fixed = lambda pair: (0, 0)
    front = lambda pair: (pair, 0, 0)
    return {
        "rows": pl.BlockSpec((rows, lanes), column),
        "row": pl.BlockSpec((1, lanes), column),
        "embed": pl.BlockSpec((2, lanes), column),
        "small": pl.BlockSpec((8, lanes), column),
        "row_code": pl.BlockSpec((rows, lanes), fixed),
        "key_code": pl.BlockSpec((keys, lanes), fixed, pipeline_mode=pl.Buffered(1)),
        "keys": pl.BlockSpec((keys, lanes), column),
        "table": pl.BlockSpec((2, blocks, 2 * lanes), front),
        "log": pl.BlockSpec((1, 1, 2 * rows), front),
        "stack": pl.BlockSpec((1, 2 * rows, 2 * lanes), front),
    }


def attention_forward(query_full, bias_content, bias_segment, embed, row_code, key_code, keys, values, table):
    rows, width = query_full.shape
    count = keys.shape[0]
    pairs = width // lanes
    spec = attention_specs(rows, count, count // lanes)
    return pl.pallas_call(
        forward_kernel,
        grid=(pairs,),
        in_specs=[
            spec["rows"],
            spec["row"],
            spec["row"],
            spec["embed"],
            spec["row_code"],
            spec["key_code"],
            spec["keys"],
            spec["keys"],
            spec["table"],
        ],
        out_specs=[spec["rows"], spec["log"], spec["stack"]],
        out_shape=[
            jax.ShapeDtypeStruct((rows, width), f32),
            jax.ShapeDtypeStruct((pairs, 1, 2 * rows), f32),
            jax.ShapeDtypeStruct((pairs, 2 * rows, 2 * lanes), bf16),
        ],
        scratch_shapes=[pltpu.VMEM((count, 2 * rows), f32)],
        compiler_params=pltpu.CompilerParams(
            dimension_semantics=("arbitrary",), vmem_limit_bytes=60 << 20
        ),
        cost_estimate=pl.CostEstimate(
            flops=4 * rows * count * width,
            bytes_accessed=4 * count * width + 8 * rows * width,
            transcendentals=rows * count * width // 64,
        ),
    )(query_full, bias_content, bias_segment, embed, row_code, key_code, keys, values, table)


def attention_backward(
    stack, query_full, bias_segment, embed, row_code, key_code, keys, values, table, out_back, attended, log_row
):
    rows, width = query_full.shape
    count = keys.shape[0]
    pairs = width // lanes
    spec = attention_specs(rows, count, count // lanes)
    return pl.pallas_call(
        backward_kernel,
        grid=(pairs,),
        in_specs=[
            spec["stack"],
            spec["rows"],
            spec["row"],
            spec["embed"],
            spec["row_code"],
            spec["key_code"],
            spec["keys"],
            spec["keys"],
            spec["table"],
            spec["rows"],
            spec["rows"],
            spec["log"],
        ],
        out_specs=[spec["rows"], spec["keys"], spec["keys"], spec["table"], spec["small"]],
        out_shape=[
            jax.ShapeDtypeStruct((rows, width), bf16),
            jax.ShapeDtypeStruct((count, width), bf16),
            jax.ShapeDtypeStruct((count, width), bf16),
            jax.ShapeDtypeStruct((2 * pairs, count // lanes, 2 * lanes), f32),
            jax.ShapeDtypeStruct((8, width), f32),
        ],
        compiler_params=pltpu.CompilerParams(
            dimension_semantics=("arbitrary",), vmem_limit_bytes=60 << 20
        ),
        cost_estimate=pl.CostEstimate(
            flops=10 * rows * count * width,
            bytes_accessed=8 * count * width + 8 * rows * width,
            transcendentals=rows * count * width // 64,
        ),
    )(stack, query_full, bias_segment, embed, row_code, key_code, keys, values, table, out_back, attended, log_row)


def body(
    content,
    query_stream,
    block_rank,
    segments,
    positions,
    query_weight,
    key_weight,
    value_weight,
    output_weight,
    content_bias,
    segment_bias,
    segment_embed,
    relative_table,
    attention_gain,
    attention_shift,
    inner_weight,
    inner_bias,
    outer_weight,
    outer_bias,
    final_gain,
    final_shift,
    content_cotangent,
    query_cotangent,
):
    block_rows = content.shape[1]
    width = content.shape[2]
    rows = 2 * block_rows
    count = lax.axis_size("ctx")
    sides = lax.axis_size("wsh")
    side = lax.axis_index("wsh")
    length = block_rows * count
    order = block_order(count)
    own_content = content[0]
    own_query = query_stream[0]
    part = width // sides
    table_heads, bucket_count = relative_table.shape
    head_count = table_heads * sides
    inner_rows = inner_bias.shape[0] // part

    table_flat = jnp.pad(
        relative_table.reshape(-1), (0, part - table_heads * bucket_count)
    ).reshape(1, part)
    small = jnp.concatenate(
        [
            jnp.stack(
                [
                    content_bias,
                    segment_bias,
                    attention_gain,
                    attention_shift,
                    outer_bias,
                    final_gain,
                    final_shift,
                ]
            ),
            segment_embed,
            inner_bias.reshape(inner_rows, part),
            table_flat,
        ],
        axis=0,
    )
    small_other = across(small)
    small_pair = jnp.where(
        side == 0, jnp.stack([small, small_other]), jnp.stack([small_other, small])
    ).astype(f32)
    vectors = jnp.transpose(small_pair[:, :9], (1, 0, 2)).reshape(9, width)
    bias_content = vectors[0:1]
    bias_segment = vectors[1:2]
    gain_first = vectors[2]
    shift_first = vectors[3]
    bias_outer = vectors[4]
    gain_second = vectors[5]
    shift_second = vectors[6]
    embed = vectors[7:9]
    bias_inner = small_pair[:, 9 : 9 + inner_rows].reshape(-1)
    table_full = small_pair[:, 9 + inner_rows, : table_heads * bucket_count].reshape(
        head_count, bucket_count
    )

    meta = jnp.concatenate(
        [
            segments[0].reshape(1, block_rows),
            jnp.broadcast_to(positions[:, :1], (1, block_rows)),
            jnp.broadcast_to(block_rank, (1, block_rows)),
        ],
        axis=0,
    )
    meta_all = jnp.stack(gather_blocks(meta))
    content_all = jnp.concatenate(gather_blocks(own_content), axis=0)

    weight_query = gather_shard(query_weight)
    weight_key = gather_shard(key_weight)
    weight_value = gather_shard(value_weight)
    weight_output = gather_shard(output_weight)
    weight_inner = gather_shard(inner_weight)
    weight_outer = gather_shard(outer_weight)

    key_segments = meta_all[:, 0, :].reshape(length)
    key_firsts = meta_all[:, 1, 0]
    key_ranks = meta_all[:, 2, 0]
    turn = jnp.arange(2 * block_rows, dtype=jnp.int32)
    turn = jnp.where(turn < block_rows, turn, turn - 2 * block_rows)
    distance = (key_firsts[0] - key_firsts)[:, None] + turn[None, :]
    number = bucket_levels(distance, length)
    onehot = (number[:, :, None] == jnp.arange(bucket_count, dtype=jnp.int32)).astype(f32)
    table = jnp.einsum("kmc,hc->hkm", onehot, table_full, precision=highest)
    table = jnp.where((key_ranks > key_ranks[0])[None, :, None], negative, table)
    lane = jnp.arange(lanes, dtype=jnp.int32)[None, :]
    key_code = jnp.where(
        lane < 8, (key_segments[:, None] == lane % 4), (lane < 10)
    ).astype(bf16)
    row_segments = jnp.concatenate([segments[0], segments[0]])
    row_code = jnp.where(
        lane < 8, (row_segments[:, None] == lane % 4), (lane < 10)
    ).astype(f32)

    streams = jnp.concatenate([own_content, own_query], axis=0)
    query_full = dot(streams, weight_query)
    keys = dot(content_all, weight_key).astype(bf16)
    values = dot(content_all, weight_value).astype(bf16)
    attended, log_row, stack = attention_forward(
        query_full, bias_content, bias_segment, embed, row_code, key_code, keys, values, table
    )

    out_low = attended.astype(bf16)
    attention_out = dot(out_low, weight_output)
    residual = streams.astype(f32) + attention_out
    normed, first_back = jax.vjp(layer_norm, residual, gain_first, shift_first)
    normed_low = normed.astype(bf16)
    inner_pre = dot(normed_low, weight_inner) + bias_inner
    active, gelu_back = jax.vjp(gelu_exact, inner_pre)
    active_low = active.astype(bf16)
    outer_out = dot(active_low, weight_outer) + bias_outer
    final_norm, second_back = jax.vjp(layer_norm, normed + outer_out, gain_second, shift_second)
    squares = jnp.stack(
        [
            jnp.sum(jnp.square(own_content.astype(f32))),
            jnp.sum(jnp.square(attention_out[:block_rows])),
            jnp.sum(jnp.square(residual[:block_rows])),
        ]
    )
    cotangent = jnp.concatenate([content_cotangent[0], query_cotangent[0]], axis=0).astype(f32)
    back_second, final_gain_back, final_shift_back = second_back(cotangent)
    outer_back = back_second.astype(bf16)
    outer_weight_back = dot_tn(active_low, outer_back).astype(bf16)
    outer_bias_back = jnp.sum(outer_back.astype(f32), axis=0)
    active_back = dot_nt(outer_back, weight_outer)
    inner_back = gelu_back(active_back)[0].astype(bf16)
    inner_weight_back = dot_tn(normed_low, inner_back).astype(bf16)
    inner_bias_back = jnp.sum(inner_back.astype(f32), axis=0)
    normed_back = back_second + dot_nt(inner_back, weight_inner)
    residual_back, first_gain_back, first_shift_back = first_back(normed_back)
    attention_back = residual_back.astype(bf16)
    output_weight_back = dot_tn(out_low, attention_back).astype(bf16)
    out_back = dot_nt(attention_back, weight_output).astype(bf16)

    outer_weight_sum = reduce_gradient(outer_weight_back)
    inner_weight_sum = reduce_gradient(inner_weight_back)
    output_weight_sum = reduce_gradient(output_weight_back)

    query_back, keys_back, values_back, diagonals, small_back = attention_backward(
        stack,
        query_full,
        bias_segment,
        embed,
        row_code,
        key_code,
        keys,
        values,
        table,
        out_back,
        attended,
        log_row,
    )
    table_back = jnp.einsum("hkm,kmc->hc", diagonals, onehot, precision=highest)
    query_weight_back = dot_tn(streams, query_back).astype(bf16)
    key_weight_back = dot_tn(content_all, keys_back).astype(bf16)
    value_weight_back = dot_tn(content_all, values_back).astype(bf16)
    query_weight_sum = reduce_gradient(query_weight_back)
    key_weight_sum = reduce_gradient(key_weight_back)
    value_weight_sum = reduce_gradient(value_weight_back)
    streams_back = residual_back + dot_nt(query_back, weight_query)
    content_share = (dot_nt(keys_back, weight_key) + dot_nt(values_back, weight_value)).astype(bf16)
    content_back = streams_back[:block_rows] + scatter_blocks(content_share)

    small_rows = jnp.concatenate(
        [
            small_back[:4],
            first_gain_back[None],
            first_shift_back[None],
            outer_bias_back[None],
            final_gain_back[None],
            final_shift_back[None],
            inner_bias_back.reshape(-1, width),
            jnp.pad(table_back.reshape(-1), (0, width - head_count * bucket_count))[None],
            jnp.pad(squares, (0, width - 3))[None],
        ],
        axis=0,
    )
    small_sum = sum_everywhere(small_rows)
    shares = lax.dynamic_slice_in_dim(small_sum[:9], side * part, part, 1)
    inner_bias_sum = lax.dynamic_slice_in_dim(
        small_sum[9 : 9 + inner_back.shape[1] // width].reshape(-1),
        side * inner_bias.shape[0],
        inner_bias.shape[0],
        0,
    )
    table_sum = lax.dynamic_slice_in_dim(
        small_sum[-2, : head_count * bucket_count].reshape(head_count, bucket_count),
        side * table_heads,
        table_heads,
        0,
    )
    token_total = length * sides * width
    root_mean = jnp.sqrt(small_sum[-1, :3] / token_total)
    return (
        final_norm[:block_rows].astype(bf16)[None],
        final_norm[block_rows:].astype(bf16)[None],
        content_back[None],
        streams_back[block_rows:][None],
        query_weight_sum,
        key_weight_sum,
        value_weight_sum,
        output_weight_sum,
        shares[0],
        shares[1],
        shares[2:4],
        table_sum,
        shares[4],
        shares[5],
        inner_weight_sum,
        inner_bias_sum,
        outer_weight_sum,
        shares[6],
        shares[7],
        shares[8],
        root_mean,
    )


def solution(mesh):
    tokens = P("wsh", "ctx", None)
    marks = P("wsh", "ctx")
    matrix = P("wsh", None)
    vector = P("wsh")
    placed = (
        (tokens, tokens, marks, marks, marks)
        + (matrix,) * 4
        + (vector, vector, P(None, "wsh"), matrix, vector, vector, matrix, vector, matrix)
        + (vector,) * 3
        + (tokens, tokens)
    )
    given = (
        (tokens,) * 4
        + (matrix,) * 4
        + (vector, vector, P(None, "wsh"), matrix, vector, vector, matrix, vector, matrix)
        + (vector,) * 3
        + (P(),)
    )
    return jax.shard_map(body, mesh=mesh, in_specs=placed, out_specs=given, check_vma=False)
```

time: 1600 us -> 588 us (0.37)
  blocking collectives: 454 us -> 0 us
  local copies, waits for them, and re-layouts: 543 us -> 93.7 us
  waiting for transfers between devices: 354 us -> 165 us
  starting transfers between devices: 0.68 us -> 138 us
  Pallas kernels: 0 us -> 59.8 us
  matrix products: 135 us -> 76.8 us
  other arithmetic: 84.2 us -> 44.9 us
    psum x2 -> x0, blocking collectives: 346 us -> none  [the longest x1 305 us: body(): lax.psum((shard_back[0], shard_back[1], shard_back[2], shard_back[3], sha...]
    reduce_scatter x6 -> x0, waiting for transfers between devices: 259 us -> none  [the longest x1 62.9 us: body(): lax.psum_scatter(outer_weight_back.astype(jnp.bfloat16), 'wsh', scatter_d...]
    ppermute x0 -> x106, waiting for transfers between devices: none -> 165 us  [the longest x92 109 us: partner(): lax.ppermute(value, 'ctx', [(place, place ^ bit) for place in range(count)])]
    reshape x13 -> x10, local copies, waits for them, and re-layouts: 161 us -> 7.14 us  [the longest x4 3.1 us: layer_norm(): return centred * lax.rsqrt(spread + epsilon) * gain_row + shift_row]
    ppermute x0 -> x106, starting transfers between devices: none -> 138 us  [the longest x92 129 us: partner(): lax.ppermute(value, 'ctx', [(place, place ^ bit) for place in range(count)])]
    all_gather x13 -> x0, blocking collectives: 101 us -> none  [the longest x1 31.6 us: body(): lax.all_gather(rank_tokens, 'ctx', axis=0, tiled=True)]
    another operation x12 -> x14, local copies, waits for them, and re-layouts: 91.6 us -> 8.74 us  [the longest x7 6.22 us: body(): jnp.stack([content_bias, segment_bias, attention_gain, attention_shift, o...]
    pallas_call x0 -> x2, Pallas kernels: none -> 59.8 us  [the longest x1 41.5 us: attention_backward(): pl.pallas_call(backward_kernel, grid=(pairs,), in_specs=[spec['stack'], s...]
  transfers between devices with their start and end apart: 17 -> 106, of which waited for: 10 -> 54; matrix products, arithmetic and copies ran while one was open for 17% -> 27% of each run, Pallas kernels for 0% -> 3%
where the time goes in v1:
time: 588 us; the launch traced here: 582 us
  waiting for transfers between devices  165 us (28%)
  starting transfers between devices  138 us (23%)
  local copies, waits for them, and re-layouts  93.7 us (16%)
  matrix products  76.8 us (13%)
  Pallas kernels  59.8 us (10%)
  other arithmetic  44.9 us (8%)
    ppermute x92, starting transfers between devices, partner(): lax.ppermute(value, 'ctx', [(place, place ^ bit) for place in range(count)])  129 us
    ppermute x92, waiting for transfers between devices, partner(): lax.ppermute(value, 'ctx', [(place, place ^ bit) for place in range(count)])  109 us
    ppermute x14, waiting for transfers between devices, across(): return lax.ppermute(value, 'wsh', [(0, 1), (1, 0)])  56 us
    pallas_call x1, Pallas kernels, attention_backward(): pl.pallas_call(backward_kernel, grid=(pairs,), in_specs=[spec['stack'], s...  41.5 us
    dot_general x6, matrix products, dot(): return jnp.dot(left, right, preferred_element_type=f32)  28.4 us
    dot_general x6, matrix products, dot_nt(): lax.dot_general(left, right, (((1,), (1,)), ((), ())), preferred_element_...  25.2 us
    unnamed x195, local copies, waits for them, and re-layouts  21.6 us
    dot_general x6, matrix products, dot_tn(): lax.dot_general(left, right, (((0,), (0,)), ((), ())), preferred_element_...  20.9 us
  transfers between devices with their start and end apart: 106, of which 54 were waited for; matrix products, arithmetic and copies ran while one was open for 27% of the time, Pallas kernels for 3%

profile of v1, /device:TPU:1, one launch (start us, length us, event | category | flops | bytes accessed | tf_op | source)
XLA Modules:
  0.0 582.3 jit_solution(605145705865515892)
XLA Ops:
  108.0 5.3 collective-permute-done
  115.0 4.7 collective-permute-done.35
  126.1 4.5 collective-permute-start.29
  142.7 6.5 %convolution_convert_fusion.2.value_ref = bf16[2048,768]{1,0:T(8,128)(2,1)} fusion(bf16[2048,768]{1,0:T(8,128)(2,1)} %constant_dynamic-update-slice_fusion.16, bf16[768,768]{1,0:T(8,128)(2,1)} %constant_dynamic-update-slice_fusion.41), kind=kOutput, calls=%fused_computation.7 | convolution fusion | flops 2417491968 | bytes 7471104 | tf_op jit(solution)/shard_map/dot_general | solution.py:43
  151.4 5.3 convolution_convert_fusion.3.key_ref
  156.6 18.3 %shard_map.382 = (f32[256,768]{1,0:T(8,128)}, f32[6,1,512]{2,1,0:T(1,128)}, bf16[6,512,256]{2,1,0:T(8,128)(2,1)}) custom-call(f32[256,768]{1,0:T(8,128)} %fusion.29.query_ref, f32[1,768]{1,0:T(1,128)} %bitcast.135, f32[1,768]{1,0:T(1,128)} %bitcast.133, f32[2,768]{1,0:T(2,128)} %bitcast.131, f32[256,128]{1,0:T(8,128)} %select_convert_fusion.1.row_code_ref, ...), custom_call_target="tpu_custom_call" | custom-call | flops 1610612736 | bytes 7864320 | tf_op jit(solution)/shard_map/pallas_call | solution.py:407
  187.3 9.7 %multiply_convert_fusion = (bf16[256,3072]{1,0:T(8,128)(2,1)S(1)}, f32[256,3072]{1,0:T(8,128)S(1)}, f32[256,3072]{1,0:T(8,128)S(1)}) fusion(f32[3072]{0:T(1024)S(1)} %copy-done.57, bf16[768,3072]{1,0:T(8,128)(2,1)} %constant_dynamic-update-slice_fusion.35, f32[256,768]{1,0:T(8,128)S(1)} %get-tuple-element.66, f32[768]{0:T(1024)S(1)} %copy-done.40, ...), kind=kOutput, calls=%fused_computation.13 | convolution fusion | flops 1260847104 | bytes 13389824 | tf_op jit(solution)/shard_map/dot_general | solution.py:43
  205.2 5.2 convert_reduce_fusion
  210.5 5.2 multiply_reduce_fusion
  217.9 41.5 %shard_map.383 = (bf16[256,768]{1,0:T(8,128)(2,1)}, bf16[2048,768]{1,0:T(8,128)(2,1)}, bf16[2048,768]{1,0:T(8,128)(2,1)}, f32[12,16,256]{2,1,0:T(8,128)}, f32[8,768]{1,0:T(8,128)}) custom-call(bf16[6,512,256]{2,1,0:T(8,128)(2,1)} %get-tuple-element.30.stack_ref, f32[256,768]{1,0:T(8,128)} %fusion.29.query_ref, f32[1,768]{1,0:T(1,128)} %bitcast.134, ...), custom_call_target="tpu_custom_call" | custom-call | flops 4026531840 | bytes 14155776 | tf_op jit(solution)/shard_map/pallas_call | solution.py:446
  259.5 6.7 %convolution_convert_fusion.5 = bf16[768,768]{1,0:T(8,128)(2,1)} fusion(bf16[2048,768]{1,0:T(8,128)(2,1)} %constant_dynamic-update-slice_fusion.16, bf16[2048,768]{1,0:T(8,128)(2,1)} %get-tuple-element.34), kind=kOutput, calls=%fused_computation.36 | convolution fusion | flops 2416508928 | bytes 7471104 | tf_op jit(solution)/shard_map/dot_general | solution.py:51
  266.2 5.9 %fusion.48 = f32[2048,768]{1,0:T(8,128)} fusion(bf16[2048,768]{1,0:T(8,128)(2,1)S(1)} %copy-done.74, bf16[768,768]{1,0:T(8,128)(2,1)} %constant_dynamic-update-slice_fusion.41), kind=kOutput, calls=%fused_computation.316 | convolution fusion | flops 2415919104 | bytes 10616832 | tf_op jit(solution)/shard_map/dot_general | solution.py:47
  298.8 4.8 convolution_convert_fusion.6
  306.1 6.2 %add_convert_fusion = bf16[2048,768]{1,0:T(8,128)(2,1)S(1)} fusion(f32[2048,768]{1,0:T(8,128)} %fusion.48, bf16[2048,768]{1,0:T(8,128)(2,1)S(1)} %copy-done.73, bf16[768,768]{1,0:T(8,128)(2,1)} %constant_dynamic-update-slice_fusion.44), kind=kOutput, calls=%fused_computation | convolution fusion | flops 2419064832 | bytes 13762560 | tf_op jit(solution)/shard_map/dot_general | solution.py:47
  343.6 5.8 collective-permute-done.48
  349.9 5.8 collective-permute-done.57
  357.1 5.0 collective-permute-done.66
  410.1 13.0 %collective-permute-start.82 = (bf16[384,384]{1,0:T(8,128)(2,1)S(1)}, bf16[384,384]{1,0:T(8,128)(2,1)S(1)}, u32[]{:S(2)}, u32[]{:S(2)}) collective-permute-start(bf16[384,384]{1,0:T(8,128)(2,1)S(1)} %maximum_select_fusion.13), channel_id=1, source_target_pairs={{0,2},{2,0},{4,6},{6,4},{8,10},{10,8},{12,14},{14,12},{16,18},{18,... | collective-permute-start | bytes 884744 | tf_op jit(solution)/shard_map/ppermute | solution.py:56
  426.6 21.3 %collective-permute-done.98 = bf16[1536,384]{1,0:T(8,128)(2,1)S(1)} collective-permute-done((bf16[1536,384]{1,0:T(8,128)(2,1)S(1)}, bf16[1536,384]{1,0:T(8,128)(2,1)S(1)}, u32[]{:S(2)}, u32[]{:S(2)}) %collective-permute-start.98) | collective-permute-done | bytes 1179680 | tf_op jit(solution)/shard_map/ppermute | solution.py:60
  449.2 12.8 %collective-permute-done.90 = bf16[192,1536]{1,0:T(8,128)(2,1)S(1)} collective-permute-done((bf16[192,1536]{1,0:T(8,128)(2,1)S(1)}, bf16[192,1536]{1,0:T(8,128)(2,1)S(1)}, u32[]{:S(2)}, u32[]{:S(2)}) %collective-permute-start.90) | collective-permute-done | bytes 589856 | tf_op jit(solution)/shard_map/ppermute | solution.py:56
  463.0 14.4 %collective-permute-done.99 = bf16[768,384]{1,0:T(8,128)(2,1)S(1)} collective-permute-done((bf16[768,384]{1,0:T(8,128)(2,1)S(1)}, bf16[768,384]{1,0:T(8,128)(2,1)S(1)}, u32[]{:S(2)}, u32[]{:S(2)}) %collective-permute-start.99) | collective-permute-done | bytes 589856 | tf_op jit(solution)/shard_map/ppermute | solution.py:56
  509.5 19.7 %collective-permute-start.55 = (bf16[384,384]{1,0:T(8,128)(2,1)S(1)}, bf16[384,384]{1,0:T(8,128)(2,1)S(1)}, u32[]{:S(2)}, u32[]{:S(2)}) collective-permute-start(bf16[384,384]{1,0:T(8,128)(2,1)S(1)} %maximum_select_fusion.10), channel_id=1, source_target_pairs={{0,2},{2,0},{4,6},{6,4},{8,10},{10,8},{12,14},{14,12},{16,18},{18,... | collective-permute-start | bytes 884744 | tf_op jit(solution)/shard_map/ppermute | solution.py:56
  549.4 5.8 %collective-permute-start.96 = (bf16[384,1536]{1,0:T(8,128)(2,1)S(1)}, bf16[384,1536]{1,0:T(8,128)(2,1)S(1)}, u32[]{:S(2)}, u32[]{:S(2)}) collective-permute-start(bf16[384,1536]{1,0:T(8,128)(2,1)S(1)} %maximum_select_fusion.2), channel_id=1, source_target_pairs={{0,2},{2,0},{4,6},{6,4},{8,10},{10,8},{12,14},{14,12},{16,18},{18,... | collective-permute-start | bytes 3538952 | tf_op jit(solution)/shard_map/ppermute | solution.py:56
  568.5 7.0 %collective-permute-done.46 = bf16[128,768]{1,0:T(8,128)(2,1)S(1)} collective-permute-done((bf16[128,768]{1,0:T(8,128)(2,1)S(1)}, bf16[128,768]{1,0:T(8,128)(2,1)S(1)}, u32[]{:S(2)}, u32[]{:S(2)}) %collective-permute-start.46) | collective-permute-done | bytes 196640 | tf_op jit(solution)/shard_map/ppermute | solution.py:56
  (619 shorter events, 338.6 us)
Async XLA Ops:
  3.6 52.4 %collective-permute-start.6 = (s32[3,128]{1,0:T(4,128)}, s32[3,128]{1,0:T(4,128)}, u32[]{:S(2)}, u32[]{:S(2)}) collective-permute-start(s32[3,128]{1,0:T(4,128)} %get-tuple-element.79), channel_id=1, source_target_pairs={{0,4},{2,6},{4,0},{6,2},{8,12},{10,14},{12,8},{14,10},{16,20},{18,... | collective-permute-start | bytes 4616 | tf_op jit(solution)/shard_map/ppermute | solution.py:56
  5.7 46.2 %collective-permute-start.5 = (s32[3,128]{1,0:T(4,128)}, s32[3,128]{1,0:T(4,128)}, u32[]{:S(2)}, u32[]{:S(2)}) collective-permute-start(s32[3,128]{1,0:T(4,128)} %get-tuple-element.79), channel_id=1, source_target_pairs={{0,24},{2,26},{4,28},{6,30},{8,16},{10,18},{12,20},{14,22},{16,8},... | collective-permute-start | bytes 4616 | tf_op jit(solution)/shard_map/ppermute | solution.py:56
  9.0 42.2 %collective-permute-start.4 = (s32[3,128]{1,0:T(4,128)}, s32[3,128]{1,0:T(4,128)}, u32[]{:S(2)}, u32[]{:S(2)}) collective-permute-start(s32[3,128]{1,0:T(4,128)} %get-tuple-element.79), channel_id=1, source_target_pairs={{0,8},{2,10},{4,12},{6,14},{8,0},{10,2},{12,4},{14,6},{16,24},{18,... | collective-permute-start | bytes 4616 | tf_op jit(solution)/shard_map/ppermute | solution.py:56
  9.0 41.4 %collective-permute-start.3 = (s32[3,128]{1,0:T(4,128)}, s32[3,128]{1,0:T(4,128)}, u32[]{:S(2)}, u32[]{:S(2)}) collective-permute-start(s32[3,128]{1,0:T(4,128)} %get-tuple-element.79), channel_id=1, source_target_pairs={{0,16},{2,18},{4,20},{6,22},{8,24},{10,26},{12,28},{14,30},{16,0},... | collective-permute-start | bytes 4616 | tf_op jit(solution)/shard_map/ppermute | solution.py:56
  9.3 55.0 %collective-permute-start.10 = (s32[3,128]{1,0:T(4,128)}, s32[3,128]{1,0:T(4,128)}, u32[]{:S(2)}, u32[]{:S(2)}) collective-permute-start(s32[3,128]{1,0:T(4,128)} %get-tuple-element.79), channel_id=1, source_target_pairs={{0,2},{2,0},{4,6},{6,4},{8,10},{10,8},{12,14},{14,12},{16,18},{18,... | collective-permute-start | bytes 4616 | tf_op jit(solution)/shard_map/ppermute | solution.py:56
  50.4 83.0 %collective-permute-start.25 = (bf16[128,768]{1,0:T(8,128)(2,1)S(1)}, bf16[128,768]{1,0:T(8,128)(2,1)}, u32[]{:S(2)}, u32[]{:S(2)}) collective-permute-start(bf16[128,768]{1,0:T(8,128)(2,1)S(1)} %bitcast.111), channel_id=1, source_target_pairs={{0,2},{2,0},{4,6},{6,4},{8,10},{10,8},{12,14},{14,12},{16,18},{18,... | collective-permute-start | bytes 589832 | tf_op jit(solution)/shard_map/ppermute | solution.py:56
  51.1 49.1 %collective-permute-start.21 = (bf16[128,768]{1,0:T(8,128)(2,1)S(1)}, bf16[128,768]{1,0:T(8,128)(2,1)}, u32[]{:S(2)}, u32[]{:S(2)}) collective-permute-start(bf16[128,768]{1,0:T(8,128)(2,1)S(1)} %bitcast.112), channel_id=1, source_target_pairs={{0,4},{2,6},{4,0},{6,2},{8,12},{10,14},{12,8},{14,10},{16,20},{18,... | collective-permute-start | bytes 589832 | tf_op jit(solution)/shard_map/ppermute | solution.py:56
  51.8 46.5 %collective-permute-start.20 = (bf16[128,768]{1,0:T(8,128)(2,1)S(1)}, bf16[128,768]{1,0:T(8,128)(2,1)}, u32[]{:S(2)}, u32[]{:S(2)}) collective-permute-start(bf16[128,768]{1,0:T(8,128)(2,1)S(1)} %bitcast.113), channel_id=1, source_target_pairs={{0,24},{2,26},{4,28},{6,30},{8,16},{10,18},{12,20},{14,22},{16,8},... | collective-permute-start | bytes 589832 | tf_op jit(solution)/shard_map/ppermute | solution.py:56
  64.2 31.3 %collective-permute-start.19 = (bf16[128,768]{1,0:T(8,128)(2,1)S(1)}, bf16[128,768]{1,0:T(8,128)(2,1)}, u32[]{:S(2)}, u32[]{:S(2)}) collective-permute-start(bf16[128,768]{1,0:T(8,128)(2,1)S(1)} %bitcast.114), channel_id=1, source_target_pairs={{0,8},{2,10},{4,12},{6,14},{8,0},{10,2},{12,4},{14,6},{16,24},{18,... | collective-permute-start | bytes 589832 | tf_op jit(solution)/shard_map/ppermute | solution.py:56
  107.0 74.4 %collective-permute-start.41 = (bf16[768,768]{1,0:T(8,128)(2,1)}, bf16[768,768]{1,0:T(8,128)(2,1)}, u32[]{:S(2)}, u32[]{:S(2)}) collective-permute-start(bf16[768,768]{1,0:T(8,128)(2,1)} %constant_dynamic-slice_fusion.32), channel_id=1, source_target_pairs={{0,1},{1,0},{2,3},{3,2},{4,5},{5,4},{6,7},{7,6},{8,9},{9,8},{10,11... | collective-permute-start | bytes 3538952 | tf_op jit(solution)/shard_map/ppermute | solution.py:60
  113.3 64.7 %collective-permute-start.39 = (bf16[192,3072]{1,0:T(8,128)(2,1)}, bf16[192,3072]{1,0:T(8,128)(2,1)}, u32[]{:S(2)}, u32[]{:S(2)}) collective-permute-start(bf16[192,3072]{1,0:T(8,128)(2,1)} %constant_dynamic-slice_fusion.33), channel_id=1, source_target_pairs={{0,1},{1,0},{2,3},{3,2},{4,5},{5,4},{6,7},{7,6},{8,9},{9,8},{10,11... | collective-permute-start | bytes 3538952 | tf_op jit(solution)/shard_map/ppermute | solution.py:60
  294.6 36.9 %collective-permute-start.74 = (bf16[768,384]{1,0:T(8,128)(2,1)}, bf16[768,384]{1,0:T(8,128)(2,1)}, u32[]{:S(2)}, u32[]{:S(2)}) collective-permute-start(bf16[768,384]{1,0:T(8,128)(2,1)} %constant_dynamic-slice_fusion.16), channel_id=1, source_target_pairs={{0,2},{2,0},{4,6},{6,4},{8,10},{10,8},{12,14},{14,12},{16,18},{18,... | collective-permute-start | bytes 1769480 | tf_op jit(solution)/shard_map/ppermute | solution.py:56
  298.8 34.1 %collective-permute-start.47 = (bf16[768,384]{1,0:T(8,128)(2,1)}, bf16[768,384]{1,0:T(8,128)(2,1)}, u32[]{:S(2)}, u32[]{:S(2)}) collective-permute-start(bf16[768,384]{1,0:T(8,128)(2,1)} %constant_dynamic-slice_fusion.31), channel_id=1, source_target_pairs={{0,2},{2,0},{4,6},{6,4},{8,10},{10,8},{12,14},{14,12},{16,18},{18,... | collective-permute-start | bytes 1769480 | tf_op jit(solution)/shard_map/ppermute | solution.py:56
  306.0 30.3 %collective-permute-start.65 = (bf16[768,384]{1,0:T(8,128)(2,1)}, bf16[768,384]{1,0:T(8,128)(2,1)}, u32[]{:S(2)}, u32[]{:S(2)}) collective-permute-start(bf16[768,384]{1,0:T(8,128)(2,1)} %constant_dynamic-slice_fusion.21), channel_id=1, source_target_pairs={{0,2},{2,0},{4,6},{6,4},{8,10},{10,8},{12,14},{14,12},{16,18},{18,... | collective-permute-start | bytes 1769480 | tf_op jit(solution)/shard_map/ppermute | solution.py:56
  325.6 84.4 %collective-permute-start.43 = (bf16[1024,768]{1,0:T(8,128)(2,1)}, bf16[1024,768]{1,0:T(8,128)(2,1)}, u32[]{:S(2)}, u32[]{:S(2)}) collective-permute-start(bf16[1024,768]{1,0:T(8,128)(2,1)} %slice.222), channel_id=1, source_target_pairs={{0,2},{2,0},{4,6},{6,4},{8,10},{10,8},{12,14},{14,12},{16,18},{18,... | collective-permute-start | bytes 4718600 | tf_op jit(solution)/shard_map/ppermute | solution.py:56
  331.5 74.7 %collective-permute-start.88 = (bf16[768,1536]{1,0:T(8,128)(2,1)}, bf16[768,1536]{1,0:T(8,128)(2,1)S(1)}, u32[]{:S(2)}, u32[]{:S(2)}) collective-permute-start(bf16[768,1536]{1,0:T(8,128)(2,1)} %constant_dynamic-slice_fusion.10), channel_id=1, source_target_pairs={{0,2},{2,0},{4,6},{6,4},{8,10},{10,8},{12,14},{14,12},{16,18},{18,... | collective-permute-start | bytes 7077896 | tf_op jit(solution)/shard_map/ppermute | solution.py:56
  332.9 74.6 %collective-permute-start.97 = (bf16[3072,384]{1,0:T(8,128)(2,1)S(1)}, bf16[3072,384]{1,0:T(8,128)(2,1)S(1)}, u32[]{:S(2)}, u32[]{:S(2)}) collective-permute-start(bf16[3072,384]{1,0:T(8,128)(2,1)S(1)} %copy-done.12), channel_id=1, source_target_pairs={{0,2},{2,0},{4,6},{6,4},{8,10},{10,8},{12,14},{14,12},{16,18},{18,... | collective-permute-start | bytes 7077896 | tf_op jit(solution)/shard_map/ppermute | solution.py:56
  405.0 103.0 %collective-permute-start.63 = (bf16[192,384]{1,0:T(8,128)(2,1)S(1)}, bf16[192,384]{1,0:T(8,128)(2,1)S(1)}, u32[]{:S(2)}, u32[]{:S(2)}) collective-permute-start(bf16[192,384]{1,0:T(8,128)(2,1)S(1)} %maximum_select_fusion.17), channel_id=1, source_target_pairs={{0,4},{2,6},{4,0},{6,2},{8,12},{10,14},{12,8},{14,10},{16,20},{18,... | collective-permute-start | bytes 442376 | tf_op jit(solution)/shard_map/ppermute | solution.py:56
  406.2 103.3 %collective-permute-start.72 = (bf16[192,384]{1,0:T(8,128)(2,1)S(1)}, bf16[192,384]{1,0:T(8,128)(2,1)S(1)}, u32[]{:S(2)}, u32[]{:S(2)}) collective-permute-start(bf16[192,384]{1,0:T(8,128)(2,1)S(1)} %maximum_select_fusion.18), channel_id=1, source_target_pairs={{0,4},{2,6},{4,0},{6,2},{8,12},{10,14},{12,8},{14,10},{16,20},{18,... | collective-permute-start | bytes 442376 | tf_op jit(solution)/shard_map/ppermute | solution.py:56
  409.3 38.6 %collective-permute-start.98 = (bf16[1536,384]{1,0:T(8,128)(2,1)S(1)}, bf16[1536,384]{1,0:T(8,128)(2,1)S(1)}, u32[]{:S(2)}, u32[]{:S(2)}) collective-permute-start(bf16[1536,384]{1,0:T(8,128)(2,1)S(1)} %constant_dynamic-slice_fusion.4), channel_id=1, source_target_pairs={{0,1},{1,0},{2,3},{3,2},{4,5},{5,4},{6,7},{7,6},{8,9},{9,8},{10,11... | collective-permute-start | bytes 3538952 | tf_op jit(solution)/shard_map/ppermute | solution.py:60
  410.1 123.4 %collective-permute-start.82 = (bf16[384,384]{1,0:T(8,128)(2,1)S(1)}, bf16[384,384]{1,0:T(8,128)(2,1)S(1)}, u32[]{:S(2)}, u32[]{:S(2)}) collective-permute-start(bf16[384,384]{1,0:T(8,128)(2,1)S(1)} %maximum_select_fusion.13), channel_id=1, source_target_pairs={{0,2},{2,0},{4,6},{6,4},{8,10},{10,8},{12,14},{14,12},{16,18},{18,... | collective-permute-start | bytes 884744 | tf_op jit(solution)/shard_map/ppermute | solution.py:56
  424.9 118.3 %collective-permute-start.44 = (bf16[512,768]{1,0:T(8,128)(2,1)S(1)}, bf16[512,768]{1,0:T(8,128)(2,1)S(1)}, u32[]{:S(2)}, u32[]{:S(2)}) collective-permute-start(bf16[512,768]{1,0:T(8,128)(2,1)S(1)} %slice.274), channel_id=1, source_target_pairs={{0,4},{2,6},{4,0},{6,2},{8,12},{10,14},{12,8},{14,10},{16,20},{18,... | collective-permute-start | bytes 2359304 | tf_op jit(solution)/shard_map/ppermute | solution.py:56
  509.5 39.9 %collective-permute-start.55 = (bf16[384,384]{1,0:T(8,128)(2,1)S(1)}, bf16[384,384]{1,0:T(8,128)(2,1)S(1)}, u32[]{:S(2)}, u32[]{:S(2)}) collective-permute-start(bf16[384,384]{1,0:T(8,128)(2,1)S(1)} %maximum_select_fusion.10), channel_id=1, source_target_pairs={{0,2},{2,0},{4,6},{6,4},{8,10},{10,8},{12,14},{14,12},{16,18},{18,... | collective-permute-start | bytes 884744 | tf_op jit(solution)/shard_map/ppermute | solution.py:56
  529.3 36.9 %collective-permute-start.64 = (bf16[384,384]{1,0:T(8,128)(2,1)S(1)}, bf16[384,384]{1,0:T(8,128)(2,1)S(1)}, u32[]{:S(2)}, u32[]{:S(2)}) collective-permute-start(bf16[384,384]{1,0:T(8,128)(2,1)S(1)} %maximum_select_fusion.11), channel_id=1, source_target_pairs={{0,2},{2,0},{4,6},{6,4},{8,10},{10,8},{12,14},{14,12},{16,18},{18,... | collective-permute-start | bytes 884744 | tf_op jit(solution)/shard_map/ppermute | solution.py:56
  (165 other events, 1464.4 us)
